TPU v7x, 512 devices: a whole 4x4x16 slice. The times are simulated.
512 devices in a mesh: dp: 16 (over x, y_lo, core), ctx: 32 (over z, y_hi).
Axes of the slice: x: 4, y: 4 (y_hi: 2, y_lo: 2; y = y_hi * 2 + y_lo), z: 16, core: 2. Of those that a mesh axis runs over, the one named last changes fastest.
Arguments:
- values: bfloat16 [16, 4096, 4096], P('dp', 'ctx'), may hold values from -6 to 6
- gate_values: bfloat16 [16, 4096, 4096], P('dp', 'ctx'), may hold values from -6 to 6
- cotangent: bfloat16 [16, 4096, 4096], P('dp', 'ctx'), may hold values from -6 to 6
- residues: float32 [8, 4096], replicated, may hold values from -0.3 to 0.3
- decay_rates: float32 [8, 4096], replicated, may hold values from 2.4414063e-05 to 0.1
Outputs:
- input_grad: bfloat16 [16, 4096, 4096], P('dp', 'ctx')
- resid_grad: float32 [8, 4096], replicated
- decay_grad: float32 [8, 4096], replicated
All inputs are finite; a program needn't handle non-finite values.
Results may differ from a plain program's by a relative error of at most 0.0013.
Values sent between devices are 32-bit elements; how exact they have to be, the bound alone decides.
No kernel may reach another device: no remote copies, remote signals or barrier semaphores. Data moves between devices by JAX's collectives and lax.ppermute only.
A program may use at most 64 MiB of HBM per device.

v0:
```python
import math

import jax
import jax.numpy as jnp
from jax import lax
from jax.sharding import PartitionSpec as P


def carried_in(x, axis, combine, identity, reverse):
    peers, place = (lax.axis_size(axis), lax.axis_index(axis))
    everything = jax.tree.map(lambda part: lax.all_gather(part, axis), x)
    start = jax.tree.map(
        lambda part, zero: jnp.broadcast_to(jnp.asarray(zero, part.dtype), part.shape), x, identity
    )

    def hop(k, before):
        at = peers - 1 - k if reverse else k
        reached = at > place if reverse else at < place
        new = combine(before, jax.tree.map(lambda part: part[at], everything))
        return jax.tree.map(lambda a, b: jnp.where(reached, a, b), new, before)

    return lax.fori_loop(0, peers, hop, start)


def on_device(values, gate_values, cotangent, residues, decay_rates):
    seq_rows, block_len, channels = values.shape
    terms = residues.shape[0]
    factor = jnp.exp(-decay_rates)
    seq_values = jnp.swapaxes(values, 0, 1)
    seq_grad = jnp.swapaxes(cotangent.astype(jnp.float32) * gate_values.astype(jnp.float32), 0, 1)
    empty = jnp.zeros((seq_rows, terms, channels), jnp.float32)
    flat = jnp.zeros((terms, channels), jnp.float32)

    def forward_step(carry, inputs):
        state_now, moment_now, sum_state, sum_moment, head_plain, head_ramp, position = carry
        value_now, grad_now = inputs
        moment_now = factor * (moment_now + state_now)
        state_now = factor * state_now + value_now.astype(jnp.float32)[:, None, :]
        position = position + 1.0
        weight_now = grad_now[:, None, :]
        sum_state = sum_state + jnp.sum(weight_now * state_now, axis=0)
        sum_moment = sum_moment + jnp.sum(weight_now * moment_now, axis=0)
        powered = jnp.exp(-decay_rates * position)
        head_plain = head_plain + weight_now * powered
        head_ramp = head_ramp + weight_now * (powered * position)
        return (
            (state_now, moment_now, sum_state, sum_moment, head_plain, head_ramp, position),
            None,
        )

    start_carry = (empty, empty, flat, flat, empty, empty, jnp.zeros((), jnp.float32))
    outcome, _ = lax.scan(forward_step, start_carry, (seq_values, seq_grad), unroll=8)
    end_state, end_moment, local_state, local_moment, head_plain, head_ramp, _ = outcome

    def backward_step(back_now, grad_now):
        back_now = factor * back_now + grad_now[:, None, :]
        return (back_now, jnp.sum(residues * back_now, axis=1))

    back_start, local_grad = lax.scan(backward_step, empty, seq_grad, reverse=True, unroll=8)
    block_size = jnp.full((), float(block_len), jnp.float32)
    nothing = jnp.zeros((), jnp.float32)

    def forward_join(earlier, later):
        early_len, early_state, early_moment = earlier
        late_len, late_state, late_moment = later
        fading = jnp.exp(-decay_rates * late_len)
        joined_state = early_state * fading + late_state
        joined_moment = fading * (early_moment + late_len * early_state) + late_moment
        return (early_len + late_len, joined_state, joined_moment)

    def backward_join(earlier, later):
        early_len, early_back = earlier
        late_len, late_back = later
        fading = jnp.exp(-decay_rates * late_len)
        return (early_len + late_len, early_back * fading + late_back)

    _, carry_state, carry_moment = carried_in(
        (block_size, end_state, end_moment), "ctx", forward_join, (nothing, empty, empty), False
    )
    _, carry_back = carried_in(
        (block_size, back_start), "ctx", backward_join, (nothing, empty), True
    )
    sum_state = local_state + jnp.sum(head_plain * carry_state, axis=0)
    sum_moment = local_moment + jnp.sum(head_ramp * carry_state + head_plain * carry_moment, axis=0)
    offsets = (block_len - jnp.arange(block_len, dtype=jnp.int32)).astype(jnp.float32)
    total_grad = local_grad
    for mode in range(terms):
        fading = jnp.exp(-decay_rates[mode][None, :] * offsets[:, None])
        weighted = residues[mode][None, :] * carry_back[:, mode, :]
        total_grad = total_grad + fading[:, None, :] * weighted[None]
    input_grad = jnp.swapaxes(total_grad, 0, 1).astype(jnp.bfloat16)
    summed_state, summed_moment = lax.psum((sum_state, sum_moment), ("dp", "ctx"))
    scale = 1.0 / math.sqrt(seq_rows * lax.axis_size("dp") * block_len * lax.axis_size("ctx"))
    resid_grad = summed_state * scale
    decay_grad = -decay_rates * residues * summed_moment * scale
    return (input_grad, resid_grad, decay_grad)


def solution(mesh):
    return jax.shard_map(
        on_device,
        mesh=mesh,
        in_specs=(P("dp", "ctx", None), P("dp", "ctx", None), P("dp", "ctx", None), P(), P()),
        out_specs=(P("dp", "ctx", None), P(), P()),
        check_vma=False,
    )
```

profile of v0, /device:TPU:6, one launch (start us, length us, event | category | flops | bytes accessed | tf_op | source)
XLA Modules:
  0.0 1090.4 jit_solution(5886143530879775874)
XLA Ops:
  8.2 1.8 convert_multiply_fusion
  10.0 3.5 reshape_transpose.7
  14.4 23.6 %while.79 = (s32[]{:T(128)}, f32[1,8,4096]{2,1,0:T(8,128)S(1)}, f32[16,8,1,4096]{3,1,2,0:T(8,128)S(1)}, f32[8,4096]{1,0:T(8,128)S(1)}, f32[16,8,1,4096]{3,2,1,0:...) while((s32[]{:T(128)}, f32[1,8,4096]{2,1,0:T(8,128)S(1)}, ...), condition=%wide.region_9.10_spmd.clone, body=%wide.region_0.9_spmd.clone.sunk | while | flops 1048587 | bytes 1573163 | solution.py:59
  39.4 49.5 %while.81 = (s32[]{:T(128)}, f32[1,8,4096]{2,1,0:T(8,128)S(1)}, f32[1,8,4096]{2,1,0:T(8,128)S(1)}, f32[8,4096]{1,0:T(8,128)S(1)}, f32[8,4096]{1,0:T(8,128)S(1)},...) while((s32[]{:T(128)}, f32[1,8,4096]{2,1,0:T(8,128)S(1)}, ...), condition=%wide.region_13.14_spmd.clone, body=%wide.region_12.13_spmd.clone.sunk | while | flops 4653074 | bytes 3457614 | solution.py:52
  93.2 84.6 %all-reduce = f32[32]{0:T(128)S(1)} all-reduce(f32[32]{0:T(128)S(1)} %dynamic-update-slice), channel_id=1, replica_groups=mesh['dp'=16,'ctx'=32] {'ctx'}, use_global_device_ids=true, to_apply=%add | all-reduce | flops 32 | bytes 256
  177.7 30.4 %all-gather.7.cloned.1.call-done = f32[32,8,4096]{2,1,0:T(8,128)} async-done(((f32[1,8,4096]{2,1,0:T(8,128)}), f32[32,8,4096]{2,1,0:T(8,128)}) %all-gather.7.cloned.1.call-update) | async-done | bytes 4194320 | tf_op jit(solution)/shard_map/all_gather | solution.py:11
  208.1 70.9 %while.80 = (s32[]{:T(128)}, f32[1,8,4096]{2,1,0:T(8,128)S(1)}, s32[]{:T(128)}, f32[32]{0:T(128)S(1)}, f32[1,8,4096]{2,1,0:T(8,128)S(1)}, /*index=5*/f32[32,1,8,...) while((s32[]{:T(128)}, f32[1,8,4096]{2,1,0:T(8,128)S(1)}, s32[]{:T(128)}, ...), condition=%wide.region_11.12_spmd.clone, body=%wide.region_10.11_spmd.clone.sunk | while | flops 163848 | bytes 524483 | solution.py:22
  279.8 90.7 %all-gather.9.cloned.1.call-done = f32[32,8,4096]{2,1,0:T(8,128)} async-done(((f32[1,8,4096]{2,1,0:T(8,128)}), f32[32,8,4096]{2,1,0:T(8,128)}) %all-gather.9.cloned.1.call-update) | async-done | bytes 4194320 | tf_op jit(solution)/shard_map/all_gather | solution.py:11
  370.6 162.4 %all-gather.11.cloned.1.call-done = f32[32,8,4096]{2,1,0:T(8,128)} async-done(((f32[1,8,4096]{2,1,0:T(8,128)}), f32[32,8,4096]{2,1,0:T(8,128)}) %all-gather.11.cloned.1.call-update) | async-done | bytes 4194320 | tf_op jit(solution)/shard_map/all_gather | solution.py:11
  533.0 94.8 %while.82 = (s32[]{:T(128)}, f32[1,8,4096]{2,1,0:T(8,128)S(1)}, f32[1,8,4096]{2,1,0:T(8,128)S(1)}, s32[]{:T(128)}, f32[32]{0:T(128)}, /*index=5*/f32[1,8,4096]{2...) while((s32[]{:T(128)}, f32[1,8,4096]{2,1,0:T(8,128)S(1)}, ...), condition=%wide.region_15.16_spmd.clone, body=%wide.region_14.15_spmd.clone.sunk | while | flops 360452 | bytes 917653 | solution.py:22
  534.4 1.7 fusion.70
  537.4 1.7 fusion.70
  540.3 1.7 fusion.70
  543.3 1.7 fusion.70
  546.2 1.7 fusion.70
  549.2 1.7 fusion.70
  552.2 1.7 fusion.70
  555.1 1.7 fusion.70
  558.1 1.7 fusion.70
  561.0 1.7 fusion.70
  564.0 1.7 fusion.70
  567.0 1.7 fusion.70
  628.7 3.7 fusion.56
  632.4 448.3 %all-reduce.4.cloned.1.call-done = (f32[8,4096]{1,0:T(8,128)}, f32[8,4096]{1,0:T(8,128)}) async-done(((f32[8,4096]{1,0:T(8,128)}, f32[8,4096]{1,0:T(8,128)}), (f32[8,4096]{1,0:T(8,128)}, f32[8,4096]{1,0:T(8,128)})) %all-reduce.4.cloned.1.call-update) | async-done | bytes 262160 | tf_op jit(solution)/shard_map/psum | solution.py:92
  (449 shorter events, 227.3 us)
Async XLA Ops:
  7.2 201.0 %all-gather.7.cloned.1.call-start = ((), (), s32[]{:S(2)}) async-start(), calls=%async_computation | async-start | bytes 4325376 | tf_op jit(solution)/shard_map/all_gather | solution.py:11
  13.5 0.9 copy-start.1
  38.0 0.7 copy-start.3
  38.0 1.4 copy-start.4
  38.6 331.9 %all-gather.9.cloned.1.call-start = ((), (), s32[]{:S(2)}) async-start(), calls=%async_computation.1 | async-start | bytes 4325376 | tf_op jit(solution)/shard_map/all_gather | solution.py:11
  39.4 51.0 %copy-start.6 = (f32[8,4096]{1,0:T(8,128)S(1)}, f32[8,4096]{1,0:T(8,128)}, u32[]{:S(2)}) copy-start(f32[8,4096]{1,0:T(8,128)} %param.17) | copy-start | bytes 393220
  88.9 0.7 copy-start
  88.9 0.7 copy-start.2
  89.6 443.4 %all-gather.11.cloned.1.call-start = ((), (), s32[]{:S(2)}) async-start(), calls=%async_computation.2 | async-start | bytes 4325376 | tf_op jit(solution)/shard_map/all_gather | solution.py:11
  90.3 990.4 %all-reduce.4.cloned.1.call-start = ((), (), s32[]{:S(2)}) async-start(), calls=%async_computation.3 | async-start | bytes 524288 | tf_op jit(solution)/shard_map/psum | solution.py:92
  279.0 253.9 %copy-start.14 = (f32[32]{0:T(128)}, f32[32]{0:T(128)S(1)}, u32[]{:S(2)}) copy-start(f32[32]{0:T(128)S(1)} %get-tuple-element.1555) | copy-start | bytes 388
  533.0 95.7 %copy-start.5 = (f32[16,8,1,4096]{3,1,2,0:T(8,128)S(1)}, f32[16,8,1,4096]{3,1,2,0:T(8,128)}, u32[]{:S(2)}) copy-start(f32[16,8,1,4096]{3,1,2,0:T(8,128)} %copy-done.4) | copy-start | bytes 6291460
  533.0 95.7 %copy-start.7 = (f32[1,4096]{1,0:T(1,128)S(1)}, f32[1,4096]{1,0:T(1,128)}, u32[]{:S(2)}) copy-start(f32[1,4096]{1,0:T(1,128)} %get-tuple-element.1042) | copy-start | bytes 49156
  533.0 95.7 %copy-start.8 = (f32[1,4096]{1,0:T(1,128)S(1)}, f32[1,4096]{1,0:T(1,128)}, u32[]{:S(2)}) copy-start(f32[1,4096]{1,0:T(1,128)} %get-tuple-element.1043) | copy-start | bytes 49156
  533.0 95.7 %copy-start.9 = (f32[1,4096]{1,0:T(1,128)S(1)}, f32[1,4096]{1,0:T(1,128)}, u32[]{:S(2)}) copy-start(f32[1,4096]{1,0:T(1,128)} %get-tuple-element.1044) | copy-start | bytes 49156
  533.0 95.7 %copy-start.10 = (f32[1,4096]{1,0:T(1,128)S(1)}, f32[1,4096]{1,0:T(1,128)}, u32[]{:S(2)}) copy-start(f32[1,4096]{1,0:T(1,128)} %get-tuple-element.1045) | copy-start | bytes 49156
  533.0 95.7 %copy-start.11 = (f32[1,4096]{1,0:T(1,128)S(1)}, f32[1,4096]{1,0:T(1,128)}, u32[]{:S(2)}) copy-start(f32[1,4096]{1,0:T(1,128)} %get-tuple-element.1046) | copy-start | bytes 49156
  533.0 95.7 %copy-start.12 = (f32[1,4096]{1,0:T(1,128)S(1)}, f32[1,4096]{1,0:T(1,128)}, u32[]{:S(2)}) copy-start(f32[1,4096]{1,0:T(1,128)} %get-tuple-element.1047) | copy-start | bytes 49156
  533.0 95.7 %copy-start.13 = (f32[1,4096]{1,0:T(1,128)S(1)}, f32[1,4096]{1,0:T(1,128)}, u32[]{:S(2)}) copy-start(f32[1,4096]{1,0:T(1,128)} %get-tuple-element.1048) | copy-start | bytes 49156
  533.0 95.7 %copy-start.15 = (f32[128]{0:T(128)S(1)}, f32[128]{0:T(128)}, u32[]{:S(2)}) copy-start(f32[128]{0:T(128)} %subtract_convert_fusion) | copy-start | bytes 1540
Sparse Core Ops, SparseCore 0:
  38.8 169.3 all-gather.6
  211.8 158.7 all-gather.8
  374.3 158.6 all-gather.10
  628.7 451.9 all-reduce.3
where the time goes:
time: 1100 us; the launch traced here: 1090 us
  waiting for transfers between devices  733 us (67%)
  other arithmetic  159 us (14%)
  local copies, waits for them, and re-layouts  97.1 us (9%)
  blocking collectives  84.6 us (8%)
  between operations  14 us (1%)
    psum x1, waiting for transfers between devices, on_device(): lax.psum((sum_state, sum_moment), ('dp', 'ctx'))  448 us
    all_gather x3, waiting for transfers between devices, carried_in(): everything = jax.tree.map(lambda part: lax.all_gather(part, axis), x)  284 us
    select_n x64, other arithmetic, hop(): return jax.tree.map(lambda a, b: jnp.where(reached, a, b), new, before)  106 us
    unnamed x1, blocking collectives  84.6 us
    dynamic_slice x64, local copies, waits for them, and re-layouts, hop(): new = combine(before, jax.tree.map(lambda part: part[at], everything))  58.6 us
  transfers between devices with their start and end apart: 4, of which 4 were waited for; matrix products, arithmetic and copies ran while one was open for 12% of the time, Pallas kernels for 0%

commit v1 on v0

v1 whole, which is shorter than its diff:
```python
import functools
import math

import jax
import jax.numpy as jnp
from jax import lax
from jax.experimental import pallas as pl
from jax.experimental.pallas import tpu as pltpu
from jax.sharding import PartitionSpec as P

F32 = jnp.float32
LANES = 128
SUBS = 8
WIDE = LANES * SUBS
NEAR = 4
SENT = 6
BACK = 3
UNROLL = 4


def rows(start, size):
    return pl.ds(pl.multiple_of(start, size), size)


def split_columns(read, scratch, length):
    for s in range(SUBS):
        scratch[pl.ds(s, length, stride=SUBS), :] = read(slice(s * LANES, (s + 1) * LANES))


def local_kernel(length, modes, values, gate, cotangent, decay, grad, sent, value_rows, decay_rows):
    split_columns(lambda c: values[0, :, c].astype(F32), value_rows, length)
    split_columns(
        lambda c: cotangent[0, :, c].astype(F32) * gate[0, :, c].astype(F32), grad, length
    )
    split_columns(lambda c: decay[:, c], decay_rows, modes)
    factor = [jnp.exp(-decay_rows[n * SUBS : (n + 1) * SUBS, :]) for n in range(modes)]
    zero = [jnp.zeros((SUBS, LANES), F32)] * modes

    def forward(t, carry):
        state, moment, sum0, sum1 = (list(part) for part in carry)
        value_now = value_rows[rows(t * SUBS, SUBS), :]
        grad_now = grad[rows(t * SUBS, SUBS), :]
        for n in range(modes):
            moment[n] = factor[n] * (moment[n] + state[n])
            state[n] = factor[n] * state[n] + value_now
            sum0[n] = sum0[n] + grad_now * state[n]
            sum1[n] = sum1[n] + grad_now * moment[n]
        return state, moment, sum0, sum1

    def backward(k, carry):
        back, ramp = (list(part) for part in carry)
        grad_now = grad[rows((length - 1 - k) * SUBS, SUBS), :]
        for n in range(modes):
            ramp[n] = factor[n] * (ramp[n] + back[n])
            back[n] = factor[n] * back[n] + grad_now
        return back, ramp

    state, moment, sum0, sum1 = lax.fori_loop(
        0, length, forward, (zero, zero, zero, zero), unroll=UNROLL
    )
    back, ramp = lax.fori_loop(0, length, backward, (zero, zero), unroll=UNROLL)
    height = SENT * modes
    for kind, part in enumerate((state, moment, back, ramp, sum0, sum1)):
        for n in range(modes):
            sent[pl.ds(kind * modes + n, SUBS, stride=height), :] = part[n]


def joined(blocks, decay, span):
    factor = jnp.exp(-decay)
    fading = jnp.exp(-decay * span)
    zero = jnp.zeros_like(decay)
    carry, ramp, total0, total1 = zero, zero, zero, zero
    carries = []
    for state, moment, back, back_ramp, sum0, sum1 in reversed(blocks):
        carries.append(carry)
        near = factor * carry
        total0 = total0 + (sum0 + state * near)
        total1 = total1 + (sum1 + moment * near + state * (factor * ramp + near))
        ramp = fading * (ramp + span * carry) + back_ramp
        carry = fading * carry + back
    all_state, all_moment = zero, zero
    for state, moment, *_ in blocks:
        all_moment = fading * (all_moment + span * all_state) + moment
        all_state = fading * all_state + state
    return carries[::-1], (all_state, all_moment, carry, ramp, total0, total1)


def near_kernel(span, modes, place, decay, data, totals, carries):
    height = SENT * modes
    first = place[0] * WIDE
    for tile in range(SUBS):
        part = lambda b, k: data[b, tile * height + k * modes : tile * height + (k + 1) * modes, :]
        here = decay[:, pl.ds(pl.multiple_of(first + tile * LANES, LANES), LANES)]
        blocks = [[part(b, k) for k in range(SENT)] for b in range(data.shape[0])]
        before, total = joined(blocks, here, span)
        for b, carry in enumerate(before):
            carries[b, tile * modes : (tile + 1) * modes, :] = carry
        for k in range(SENT):
            totals[tile, k * modes : (k + 1) * modes, :] = total[k]


def far_kernel(span, modes, place, decay, data, carries, sums):
    here = decay[:, pl.ds(pl.multiple_of(place[1] * LANES, LANES), LANES)]
    blocks = [
        [data[b, k * modes : (k + 1) * modes, :] for k in range(SENT)] for b in range(data.shape[0])
    ]
    before, total = joined(blocks, here, span)
    for b, carry in enumerate(before):
        carries[b] = carry
    for d in range(sums.shape[0]):
        sums[d, :modes, :] = total[4]
        sums[d, modes:, :] = total[5]


def sum_kernel(modes, carries, sums, out):
    total = sums[0]
    for d in range(1, sums.shape[0]):
        total = total + sums[d]
    for b in range(out.shape[0]):
        out[b, :modes, :] = carries[b]
        out[b, modes:, :] = total


def spread_kernel(span, modes, place, decay, carries, far, out):
    height = BACK * modes
    first = place[0] * WIDE
    blocks = carries.shape[0]
    for tile in range(SUBS):
        here = decay[:, pl.ds(pl.multiple_of(first + tile * LANES, LANES), LANES)]
        fading = jnp.exp(-here * span)
        arriving = far[tile, :modes, :]
        for b in reversed(range(blocks)):
            start = tile * height
            out[b, start : start + modes, :] = (
                carries[b, tile * modes : (tile + 1) * modes, :] + arriving
            )
            out[b, start + modes : start + height, :] = far[tile, modes:, :]
            arriving = fading * arriving


def final_kernel(length, modes, scale, grad, arrived, decay, residues, input_grad, resid_grad,
                 decay_grad, total_rows, decay_rows, residue_rows):
    height = BACK * modes
    split_columns(lambda c: decay[:, c], decay_rows, modes)
    split_columns(lambda c: residues[:, c], residue_rows, modes)
    factor = [jnp.exp(-decay_rows[n * SUBS : (n + 1) * SUBS, :]) for n in range(modes)]
    weight = [residue_rows[n * SUBS : (n + 1) * SUBS, :] for n in range(modes)]
    start = [arrived[pl.ds(n, SUBS, stride=height), :] for n in range(modes)]

    def backward(k, back):
        at = rows((length - 1 - k) * SUBS, SUBS)
        grad_now = grad[at, :]
        back = [factor[n] * back[n] + grad_now for n in range(modes)]
        terms = [weight[n] * back[n] for n in range(modes)]
        while len(terms) > 1:
            terms = [a + b for a, b in zip(terms[::2], terms[1::2])]
        total_rows[at, :] = terms[0]
        return back

    lax.fori_loop(0, length, backward, start, unroll=UNROLL)
    for s in range(SUBS):
        cols = slice(s * LANES, (s + 1) * LANES)
        input_grad[0, :, cols] = total_rows[pl.ds(s, length, stride=SUBS), :].astype(jnp.bfloat16)
        at = s * height
        resid_grad[:, cols] = arrived[at + modes : at + 2 * modes, :] * scale
        decay_grad[:, cols] = (
            -decay[:, cols] * residues[:, cols] * arrived[at + 2 * modes : at + 3 * modes, :] * scale
        )


def on_device(values, gate_values, cotangent, residues, decay_rates):
    _, length, channels = values.shape
    modes = residues.shape[0]
    peers, rows_of = lax.axis_size("ctx"), lax.axis_size("dp")
    far = peers // NEAR
    wide = channels // WIDE
    assert modes == SUBS and wide == NEAR and far == SUBS and values.shape[0] == 1
    me = lax.axis_index("ctx")
    place = jnp.stack([me % NEAR, (me % NEAR) * SUBS + me // NEAR]).astype(jnp.int32)
    near_groups = [[g * NEAR + k for k in range(NEAR)] for g in range(far)]
    far_groups = [[k * NEAR + g for k in range(far)] for g in range(NEAR)]
    shape = lambda *dims: jax.ShapeDtypeStruct(dims, F32)
    vmem = pl.BlockSpec(memory_space=pltpu.VMEM)
    smem = pl.BlockSpec(memory_space=pltpu.SMEM)

    data = pl.BlockSpec((1, length, WIDE), lambda q: (0, 0, q))
    table = pl.BlockSpec((modes, WIDE), lambda q: (0, q))
    flat = lambda size: pl.BlockSpec((size, LANES), lambda q: (q, 0))
    grad, sent = pl.pallas_call(
        functools.partial(local_kernel, length, modes),
        grid=(wide,),
        in_specs=[data, data, data, table],
        out_specs=[flat(length * SUBS), flat(SUBS * SENT * modes)],
        out_shape=[shape(wide * length * SUBS, LANES), shape(wide * SUBS * SENT * modes, LANES)],
        scratch_shapes=[
            pltpu.VMEM((length * SUBS, LANES), F32),
            pltpu.VMEM((modes * SUBS, LANES), F32),
        ],
        name="local",
    )(values, gate_values, cotangent, decay_rates)

    def exchange(x, axis, groups):
        return lax.all_to_all(x, axis, 0, 0, tiled=True, axis_index_groups=groups)

    near_data = exchange(sent.reshape(NEAR, SUBS * SENT * modes, LANES), "ctx", near_groups)
    totals, near_carries = pl.pallas_call(
        functools.partial(near_kernel, float(length), modes),
        in_specs=[smem, vmem, vmem],
        out_specs=[vmem, vmem],
        out_shape=[shape(far, SENT * modes, LANES), shape(NEAR, SUBS * modes, LANES)],
        name="near",
    )(place, decay_rates, near_data)

    far_data = exchange(totals, "ctx", far_groups)
    far_carries, sums = pl.pallas_call(
        functools.partial(far_kernel, float(length * NEAR), modes),
        in_specs=[smem, vmem, vmem],
        out_specs=[vmem, vmem],
        out_shape=[shape(far, modes, LANES), shape(rows_of, 2 * modes, LANES)],
        name="far",
    )(place, decay_rates, far_data)

    all_sums = exchange(sums, "dp", None)
    far_out = pl.pallas_call(
        functools.partial(sum_kernel, modes),
        in_specs=[vmem, vmem],
        out_specs=vmem,
        out_shape=shape(far, BACK * modes, LANES),
        name="sum",
    )(far_carries, all_sums)

    far_back = exchange(far_out, "ctx", far_groups)
    near_out = pl.pallas_call(
        functools.partial(spread_kernel, float(length), modes),
        in_specs=[smem, vmem, vmem, vmem],
        out_specs=vmem,
        out_shape=shape(NEAR, SUBS * BACK * modes, LANES),
        name="spread",
    )(place, decay_rates, near_carries, far_back)

    arrived = exchange(near_out, "ctx", near_groups)
    scale = 1.0 / math.sqrt(rows_of * length * peers)
    return pl.pallas_call(
        functools.partial(final_kernel, length, modes, scale),
        grid=(wide,),
        in_specs=[flat(length * SUBS), flat(SUBS * BACK * modes), table, table],
        out_specs=[data, table, table],
        out_shape=[
            jax.ShapeDtypeStruct(values.shape, jnp.bfloat16),
            shape(modes, channels),
            shape(modes, channels),
        ],
        scratch_shapes=[
            pltpu.VMEM((length * SUBS, LANES), F32),
            pltpu.VMEM((modes * SUBS, LANES), F32),
            pltpu.VMEM((modes * SUBS, LANES), F32),
        ],
        name="final",
    )(grad, arrived.reshape(-1, LANES), decay_rates, residues)


def solution(mesh):
    return jax.shard_map(
        on_device,
        mesh=mesh,
        in_specs=(P("dp", "ctx", None), P("dp", "ctx", None), P("dp", "ctx", None), P(), P()),
        out_specs=(P("dp", "ctx", None), P(), P()),
        check_vma=False,
    )
```

time: 1100 us -> 118 us (0.11)
  waiting for transfers between devices: 733 us -> 11.7 us
  other arithmetic: 159 us -> 0.58 us
  local copies, waits for them, and re-layouts: 97.1 us -> 0.88 us
  Pallas kernels: 0 us -> 24.5 us
  between operations: 14 us -> 0.64 us
  blocking collectives: 84.6 us -> 72.8 us
    psum x1 -> x0, waiting for transfers between devices: 448 us -> none  [on_device(): lax.psum((sum_state, sum_moment), ('dp', 'ctx'))]
    all_gather x3 -> x0, waiting for transfers between devices: 284 us -> none  [carried_in(): everything = jax.tree.map(lambda part: lax.all_gather(part, axis), x)]
    select_n x64 -> x0, other arithmetic: 106 us -> none  [hop(): return jax.tree.map(lambda a, b: jnp.where(reached, a, b), new, before)]
    unnamed x1 -> x0, blocking collectives: 84.6 us -> none
    all_to_all x0 -> x4, blocking collectives: none -> 72.8 us  [exchange(): return lax.all_to_all(x, axis, 0, 0, tiled=True, axis_index_groups=groups)]
    dynamic_slice x64 -> x0, local copies, waits for them, and re-layouts: 58.6 us -> none  [hop(): new = combine(before, jax.tree.map(lambda part: part[at], everything))]
    slice x32 -> x0, local copies, waits for them, and re-layouts: 27.6 us -> none  [the longest x16 13.8 us: on_device(): lax.scan(forward_step, start_carry, (seq_values, seq_grad), unroll=8)]
    convert_element_type x18 -> x0, other arithmetic: 26 us -> none  [the longest x16 21.7 us: forward_step(): state_now = factor * state_now + value_now.astype(jnp.float32)[:, None, :]]
  transfers between devices with their start and end apart: 4 -> 1, of which waited for: 4 -> 1; matrix products, arithmetic and copies ran while one was open for 12% -> 0% of each run, Pallas kernels for 0% -> 0%
where the time goes in v1:
time: 118 us; the launch traced here: 117 us
  blocking collectives  72.8 us (62%)
  Pallas kernels  24.5 us (21%)
  waiting for transfers between devices  11.7 us (10%)
  starting transfers between devices  5.82 us (5%)
    all_to_all x4, blocking collectives, exchange(): return lax.all_to_all(x, axis, 0, 0, tiled=True, axis_index_groups=groups)  72.8 us
    pallas_call x1, Pallas kernels, on_device(): pl.pallas_call(functools.partial(local_kernel, length, modes), grid=(wide...  11.7 us
    all_to_all x1, waiting for transfers between devices, exchange(): return lax.all_to_all(x, axis, 0, 0, tiled=True, axis_index_groups=groups)  11.7 us
    all_to_all x1, starting transfers between devices, exchange(): return lax.all_to_all(x, axis, 0, 0, tiled=True, axis_index_groups=groups)  5.82 us
    pallas_call x1, Pallas kernels, on_device(): pl.pallas_call(functools.partial(final_kernel, length, modes, scale), gri...  5.58 us
  transfers between devices with their start and end apart: 1, of which 1 were waited for; matrix products, arithmetic and copies ran while one was open for 0% of the time, Pallas kernels for 0%

profile of v1, /device:TPU:6, one launch (start us, length us, event | category | flops | bytes accessed | tf_op | source)
XLA Modules:
  0.0 116.9 jit_solution(1526165244336344818)
XLA Ops:
  0.6 11.7 %local.1 = (f32[4096,128]{1,0:T(8,128)}, f32[1536,128]{1,0:T(8,128)}) custom-call(bf16[1,128,4096]{2,1,0:T(8,128)(2,1)} %values.1, bf16[1,128,4096]{2,1,0:T(8,128)(2,1)} %gate.1, bf16[1,128,4096]{2,1,0:T(8,128)(2,1)} %cotangent.1, f32[8,4096]{1,0:T(8,128)} %decay.9), custom_call_target="tpu_custom_call" | custom-call | tf_op jit(solution)/shard_map/local/pallas_call | solution.py:189
  12.4 5.8 %all-to-all-start = ((f32[4,384,128]{2,1,0:T(8,128)}), f32[4,384,128]{2,1,0:T(8,128)S(1)}, u32[]{:S(2)}, u32[]{:S(2)}) async-start(f32[4,384,128]{2,1,0:T(8,128)} %bitcast.5), calls=%async_computation | async-start | bytes 1572864 | tf_op jit(solution)/shard_map/all_to_all | solution.py:203
  18.2 0.6 pad_add_fusion.place
  18.8 11.7 %all-to-all-done.data = f32[4,384,128]{2,1,0:T(8,128)S(1)} async-done(((f32[4,384,128]{2,1,0:T(8,128)}), f32[4,384,128]{2,1,0:T(8,128)S(1)}, u32[]{:S(2)}, u32[]{:S(2)}) %all-to-all-start) | async-done | bytes 786464 | tf_op jit(solution)/shard_map/all_to_all | solution.py:203
  30.5 0.0 copy-start
  30.5 0.9 copy-done
  31.3 2.1 %near.1 = (f32[8,48,128]{2,1,0:T(8,128)}, f32[4,64,128]{2,1,0:T(8,128)}) custom-call(s32[2]{0:T(128)} %pad_add_fusion.place, f32[8,4096]{1,0:T(8,128)} %decay.9, f32[4,384,128]{2,1,0:T(8,128)} %copy-done), custom_call_target="tpu_custom_call" | custom-call | tf_op jit(solution)/shard_map/near/pallas_call | solution.py:206
  33.4 32.7 %all_to_all.25.data = f32[8,48,128]{2,1,0:T(8,128)} all-to-all(f32[8,48,128]{2,1,0:T(8,128)} %get-tuple-element.12), channel_id=1, replica_groups={{0,4,8,12,16,20,24,28},{1,5,9,13,17,21,25,29},{2,6,10,14,18,22,26,30},{..., dimensions={0} | all-to-all | bytes 393216 | tf_op jit(solution)/shard_map/all_to_all | solution.py:203
  66.1 1.7 %far.1 = (f32[8,8,128]{2,1,0:T(8,128)}, f32[16,16,128]{2,1,0:T(8,128)}) custom-call(s32[2]{0:T(128)} %pad_add_fusion.place, f32[8,4096]{1,0:T(8,128)} %decay.9, f32[8,48,128]{2,1,0:T(8,128)} %all_to_all.25.data), custom_call_target="tpu_custom_call" | custom-call | tf_op jit(solution)/shard_map/far/pallas_call | solution.py:215
  67.8 9.4 %all_to_all.26.sums = f32[16,16,128]{2,1,0:T(8,128)} all-to-all(f32[16,16,128]{2,1,0:T(8,128)} %get-tuple-element.14), channel_id=1, replica_groups=mesh['dp'=16,'ctx'=32] {'dp'}, dimensions={0} | all-to-all | bytes 262144 | tf_op jit(solution)/shard_map/all_to_all | solution.py:203
  77.2 1.6 %sum.1 = f32[8,24,128]{2,1,0:T(8,128)} custom-call(f32[8,8,128]{2,1,0:T(8,128)} %get-tuple-element.13.carries, f32[16,16,128]{2,1,0:T(8,128)} %all_to_all.26.sums), custom_call_target="tpu_custom_call" | custom-call | tf_op jit(solution)/shard_map/sum/pallas_call | solution.py:224
  78.8 18.6 %all_to_all.27.far = f32[8,24,128]{2,1,0:T(8,128)} all-to-all(f32[8,24,128]{2,1,0:T(8,128)} %sum.1), channel_id=1, replica_groups={{0,4,8,12,16,20,24,28},{1,5,9,13,17,21,25,29},{2,6,10,14,18,22,26,30},{..., dimensions={0} | all-to-all | bytes 196608 | tf_op jit(solution)/shard_map/all_to_all | solution.py:203
  97.4 1.8 %spread.1 = f32[4,192,128]{2,1,0:T(8,128)} custom-call(s32[2]{0:T(128)} %pad_add_fusion.place, f32[8,4096]{1,0:T(8,128)} %decay.9, f32[4,64,128]{2,1,0:T(8,128)} %get-tuple-element.11.carries, f32[8,24,128]{2,1,0:T(8,128)} %all_to_all.27.far), custom_call_target="tpu_custom_call" | custom-call | tf_op jit(solution)/shard_map/spread/pallas_call | solution.py:233
  99.2 12.1 %all_to_all.28 = f32[4,192,128]{2,1,0:T(8,128)} all-to-all(f32[4,192,128]{2,1,0:T(8,128)} %spread.1), channel_id=1, replica_groups={{0,1,2,3},{4,5,6,7},{8,9,10,11},{12,13,14,15},{16,17,18,19},{20,21,22,2..., dimensions={0} | all-to-all | bytes 786432 | tf_op jit(solution)/shard_map/all_to_all | solution.py:203
  111.3 5.6 %final.1 = (bf16[1,128,4096]{2,1,0:T(8,128)(2,1)}, f32[8,4096]{1,0:T(8,128)}, f32[8,4096]{1,0:T(8,128)}) custom-call(f32[4096,128]{1,0:T(8,128)} %get-tuple-element.9.grad, f32[768,128]{1,0:T(8,128)} %bitcast.4, f32[8,4096]{1,0:T(8,128)} %decay.9, f32[8,4096]{1,0:T(8,128)} %residues.1), custom_call_target="tpu_custom_call" | custom-call | tf_op jit(solution)/shard_map/final/pallas_call | solution.py:243
Async XLA Ops:
  12.4 18.1 %all-to-all-start = ((f32[4,384,128]{2,1,0:T(8,128)}), f32[4,384,128]{2,1,0:T(8,128)S(1)}, u32[]{:S(2)}, u32[]{:S(2)}) async-start(f32[4,384,128]{2,1,0:T(8,128)} %bitcast.5), calls=%async_computation | async-start | bytes 1572864 | tf_op jit(solution)/shard_map/all_to_all | solution.py:203
  30.5 0.9 copy-start

commit v2 on v1

--- a/solution.py
+++ b/solution.py
@@ -60,9 +60,10 @@
     )
     back, ramp = lax.fori_loop(0, length, backward, (zero, zero), unroll=UNROLL)
     height = SENT * modes
+    first = pl.multiple_of(pl.program_id(0) * SUBS * height, SUBS * height)
     for kind, part in enumerate((state, moment, back, ramp, sum0, sum1)):
         for n in range(modes):
-            sent[pl.ds(kind * modes + n, SUBS, stride=height), :] = part[n]
+            sent[pl.ds(first + kind * modes + n, SUBS, stride=height), :] = part[n]
 
 
 def joined(blocks, decay, span):
@@ -138,33 +139,57 @@
             arriving = fading * arriving
 
 
-def final_kernel(length, modes, scale, grad, arrived, decay, residues, input_grad, resid_grad,
-                 decay_grad, total_rows, decay_rows, residue_rows):
-    height = BACK * modes
+def inner_kernel(length, modes, grad, decay, residues, total, decay_rows, residue_rows):
     split_columns(lambda c: decay[:, c], decay_rows, modes)
     split_columns(lambda c: residues[:, c], residue_rows, modes)
     factor = [jnp.exp(-decay_rows[n * SUBS : (n + 1) * SUBS, :]) for n in range(modes)]
     weight = [residue_rows[n * SUBS : (n + 1) * SUBS, :] for n in range(modes)]
-    start = [arrived[pl.ds(n, SUBS, stride=height), :] for n in range(modes)]
 
     def backward(k, back):
         at = rows((length - 1 - k) * SUBS, SUBS)
         grad_now = grad[at, :]
         back = [factor[n] * back[n] + grad_now for n in range(modes)]
-        terms = [weight[n] * back[n] for n in range(modes)]
-        while len(terms) > 1:
-            terms = [a + b for a, b in zip(terms[::2], terms[1::2])]
-        total_rows[at, :] = terms[0]
+        total[at, :] = pairwise([weight[n] * back[n] for n in range(modes)])
         return back
+
+    lax.fori_loop(
+        0, length, backward, [jnp.zeros((SUBS, LANES), F32)] * modes, unroll=UNROLL
+    )
+
+
+def pairwise(terms):
+    while len(terms) > 1:
+        terms = [a + b for a, b in zip(terms[::2], terms[1::2])]
+    return terms[0]
+
+
+def final_kernel(length, modes, scale, inner, arrived, decay, residues, input_grad, resid_grad,
+                 decay_grad, total_rows, decay_rows, residue_rows):
+    height = BACK * modes
+    first = pl.multiple_of(pl.program_id(0) * SUBS * height, SUBS * height)
+    split_columns(lambda c: decay[:, c], decay_rows, modes)
+    split_columns(lambda c: residues[:, c], residue_rows, modes)
+    factor = [jnp.exp(-decay_rows[n * SUBS : (n + 1) * SUBS, :]) for n in range(modes)]
+    start = [
+        residue_rows[n * SUBS : (n + 1) * SUBS, :]
+        * arrived[pl.ds(first + n, SUBS, stride=height), :]
+        for n in range(modes)
+    ]
+
+    def backward(k, tail):
+        at = rows((length - 1 - k) * SUBS, SUBS)
+        tail = [factor[n] * tail[n] for n in range(modes)]
+        total_rows[at, :] = inner[at, :] + pairwise(tail)
+        return tail
 
     lax.fori_loop(0, length, backward, start, unroll=UNROLL)
     for s in range(SUBS):
         cols = slice(s * LANES, (s + 1) * LANES)
         input_grad[0, :, cols] = total_rows[pl.ds(s, length, stride=SUBS), :].astype(jnp.bfloat16)
-        at = s * height
-        resid_grad[:, cols] = arrived[at + modes : at + 2 * modes, :] * scale
+        at = first + s * height
+        resid_grad[:, cols] = arrived[rows(at + modes, modes), :] * scale
         decay_grad[:, cols] = (
-            -decay[:, cols] * residues[:, cols] * arrived[at + 2 * modes : at + 3 * modes, :] * scale
+            -decay[:, cols] * residues[:, cols] * arrived[rows(at + 2 * modes, modes), :] * scale
         )
 
 
@@ -182,7 +207,10 @@
     shape = lambda *dims: jax.ShapeDtypeStruct(dims, F32)
     vmem = pl.BlockSpec(memory_space=pltpu.VMEM)
     smem = pl.BlockSpec(memory_space=pltpu.SMEM)
-
+    on_chip = lambda x: pltpu.with_memory_space_constraint(x, pltpu.VMEM)
+    held = lambda *dims: pltpu.VMEM(dims, F32)
+
+    near_decay = on_chip(decay_rates)
     data = pl.BlockSpec((1, length, WIDE), lambda q: (0, 0, q))
     table = pl.BlockSpec((modes, WIDE), lambda q: (0, q))
     flat = lambda size: pl.BlockSpec((size, LANES), lambda q: (q, 0))
@@ -190,8 +218,8 @@
         functools.partial(local_kernel, length, modes),
         grid=(wide,),
         in_specs=[data, data, data, table],
-        out_specs=[flat(length * SUBS), flat(SUBS * SENT * modes)],
-        out_shape=[shape(wide * length * SUBS, LANES), shape(wide * SUBS * SENT * modes, LANES)],
+        out_specs=[flat(length * SUBS), vmem],
+        out_shape=[shape(wide * length * SUBS, LANES), held(wide * SUBS * SENT * modes, LANES)],
         scratch_shapes=[
             pltpu.VMEM((length * SUBS, LANES), F32),
             pltpu.VMEM((modes * SUBS, LANES), F32),
@@ -203,47 +231,64 @@
         return lax.all_to_all(x, axis, 0, 0, tiled=True, axis_index_groups=groups)
 
     near_data = exchange(sent.reshape(NEAR, SUBS * SENT * modes, LANES), "ctx", near_groups)
+    inner = pl.pallas_call(
+        functools.partial(inner_kernel, length, modes),
+        grid=(wide,),
+        in_specs=[flat(length * SUBS), table, table],
+        out_specs=flat(length * SUBS),
+        out_shape=shape(wide * length * SUBS, LANES),
+        scratch_shapes=[
+            pltpu.VMEM((modes * SUBS, LANES), F32),
+            pltpu.VMEM((modes * SUBS, LANES), F32),
+        ],
+        cost_estimate=pl.CostEstimate(
+            flops=4 * modes * length * channels,
+            bytes_accessed=8 * length * channels,
+            transcendentals=0,
+        ),
+        name="inner",
+    )(grad, decay_rates, residues)
     totals, near_carries = pl.pallas_call(
         functools.partial(near_kernel, float(length), modes),
         in_specs=[smem, vmem, vmem],
         out_specs=[vmem, vmem],
-        out_shape=[shape(far, SENT * modes, LANES), shape(NEAR, SUBS * modes, LANES)],
+        out_shape=[held(far, SENT * modes, LANES), held(NEAR, SUBS * modes, LANES)],
         name="near",
-    )(place, decay_rates, near_data)
+    )(place, near_decay, on_chip(near_data))
 
     far_data = exchange(totals, "ctx", far_groups)
     far_carries, sums = pl.pallas_call(
         functools.partial(far_kernel, float(length * NEAR), modes),
         in_specs=[smem, vmem, vmem],
         out_specs=[vmem, vmem],
-        out_shape=[shape(far, modes, LANES), shape(rows_of, 2 * modes, LANES)],
+        out_shape=[held(far, modes, LANES), held(rows_of, 2 * modes, LANES)],
         name="far",
-    )(place, decay_rates, far_data)
+    )(place, near_decay, on_chip(far_data))
 
     all_sums = exchange(sums, "dp", None)
     far_out = pl.pallas_call(
         functools.partial(sum_kernel, modes),
         in_specs=[vmem, vmem],
         out_specs=vmem,
-        out_shape=shape(far, BACK * modes, LANES),
+        out_shape=held(far, BACK * modes, LANES),
         name="sum",
-    )(far_carries, all_sums)
+    )(on_chip(far_carries), on_chip(all_sums))
 
     far_back = exchange(far_out, "ctx", far_groups)
     near_out = pl.pallas_call(
         functools.partial(spread_kernel, float(length), modes),
         in_specs=[smem, vmem, vmem, vmem],
         out_specs=vmem,
-        out_shape=shape(NEAR, SUBS * BACK * modes, LANES),
+        out_shape=held(NEAR, SUBS * BACK * modes, LANES),
         name="spread",
-    )(place, decay_rates, near_carries, far_back)
+    )(place, near_decay, on_chip(near_carries), on_chip(far_back))
 
     arrived = exchange(near_out, "ctx", near_groups)
     scale = 1.0 / math.sqrt(rows_of * length * peers)
     return pl.pallas_call(
         functools.partial(final_kernel, length, modes, scale),
         grid=(wide,),
-        in_specs=[flat(length * SUBS), flat(SUBS * BACK * modes), table, table],
+        in_specs=[flat(length * SUBS), vmem, table, table],
         out_specs=[data, table, table],
         out_shape=[
             jax.ShapeDtypeStruct(values.shape, jnp.bfloat16),
@@ -256,7 +301,7 @@
             pltpu.VMEM((modes * SUBS, LANES), F32),
         ],
         name="final",
-    )(grad, arrived.reshape(-1, LANES), decay_rates, residues)
+    )(inner, on_chip(arrived.reshape(-1, LANES)), decay_rates, residues)
 
 
 def solution(mesh):

time: 118 us -> 110 us (0.932)
  blocking collectives: 72.8 us -> 58.9 us
  starting transfers between devices: 5.82 us -> 9.35 us
  waiting for transfers between devices: 11.7 us -> 13.7 us
    all_to_all x4 -> x3, blocking collectives: 72.8 us -> 58.9 us  [exchange(): return lax.all_to_all(x, axis, 0, 0, tiled=True, axis_index_groups=groups)]
    pallas_call x0 -> x1, Pallas kernels: none -> 5.31 us  [on_device(): pl.pallas_call(functools.partial(inner_kernel, length, modes), grid=(wide...]
    all_to_all x1 -> x2, starting transfers between devices: 5.82 us -> 9.35 us  [exchange(): return lax.all_to_all(x, axis, 0, 0, tiled=True, axis_index_groups=groups)]
    all_to_all x1 -> x2, waiting for transfers between devices: 11.7 us -> 13.7 us  [exchange(): return lax.all_to_all(x, axis, 0, 0, tiled=True, axis_index_groups=groups)]
    pallas_call x1, Pallas kernels: 1.59 us -> 0.02 us  [on_device(): pl.pallas_call(functools.partial(sum_kernel, modes), in_specs=[vmem, vmem...]
    pallas_call x1, Pallas kernels: 2.05 us -> 0.77 us  [on_device(): pl.pallas_call(functools.partial(near_kernel, float(length), modes), in_s...]
  transfers between devices with their start and end apart: 1 -> 2, of which waited for: 1 -> 2; matrix products, arithmetic and copies ran while one was open for 0% -> 1% of each run, Pallas kernels for 0% -> 5%
where the time goes in v2:
time: 110 us; the launch traced here: 108 us
  blocking collectives  58.9 us (54%)
  Pallas kernels  24.9 us (23%)
  waiting for transfers between devices  13.7 us (12%)
  starting transfers between devices  9.35 us (8%)
    all_to_all x3, blocking collectives, exchange(): return lax.all_to_all(x, axis, 0, 0, tiled=True, axis_index_groups=groups)  58.9 us
    all_to_all x2, waiting for transfers between devices, exchange(): return lax.all_to_all(x, axis, 0, 0, tiled=True, axis_index_groups=groups)  13.7 us
    pallas_call x1, Pallas kernels, on_device(): pl.pallas_call(functools.partial(local_kernel, length, modes), grid=(wide...  12.1 us
    all_to_all x2, starting transfers between devices, exchange(): return lax.all_to_all(x, axis, 0, 0, tiled=True, axis_index_groups=groups)  9.35 us
    pallas_call x1, Pallas kernels, on_device(): pl.pallas_call(functools.partial(inner_kernel, length, modes), grid=(wide...  5.31 us
    pallas_call x1, Pallas kernels, on_device(): pl.pallas_call(functools.partial(final_kernel, length, modes, scale), gri...  4.63 us
  transfers between devices with their start and end apart: 2, of which 2 were waited for; matrix products, arithmetic and copies ran while one was open for 1% of the time, Pallas kernels for 5%

profile of v2, /device:TPU:6, one launch (start us, length us, event | category | flops | bytes accessed | tf_op | source)
XLA Modules:
  0.0 108.2 jit_solution(15278396676745080204)
XLA Ops:
  0.6 0.0 copy-start
  0.6 12.1 %local.1 = (f32[4096,128]{1,0:T(8,128)}, f32[1536,128]{1,0:T(8,128)}) custom-call(bf16[1,128,4096]{2,1,0:T(8,128)(2,1)} %values.1, bf16[1,128,4096]{2,1,0:T(8,128)(2,1)} %gate.1, bf16[1,128,4096]{2,1,0:T(8,128)(2,1)} %cotangent.1, f32[8,4096]{1,0:T(8,128)} %decay.11), custom_call_target="tpu_custom_call" | custom-call | tf_op jit(solution)/shard_map/local/pallas_call | solution.py:217
  12.7 5.8 %all-to-all-start = ((f32[4,384,128]{2,1,0:T(8,128)}), f32[4,384,128]{2,1,0:T(8,128)S(1)}, u32[]{:S(2)}, u32[]{:S(2)}) async-start(f32[4,384,128]{2,1,0:T(8,128)} %bitcast.2), calls=%async_computation | async-start | bytes 1572864 | tf_op jit(solution)/shard_map/all_to_all | solution.py:231
  18.5 0.7 pad_add_fusion.place
  19.2 11.6 %all-to-all-done.data = f32[4,384,128]{2,1,0:T(8,128)S(1)} async-done(((f32[4,384,128]{2,1,0:T(8,128)}), f32[4,384,128]{2,1,0:T(8,128)S(1)}, u32[]{:S(2)}, u32[]{:S(2)}) %all-to-all-start) | async-done | bytes 786464 | tf_op jit(solution)/shard_map/all_to_all | solution.py:231
  30.8 0.0 copy-done
  30.8 0.8 near.1
  31.6 32.4 %all_to_all.25.data = f32[8,48,128]{2,1,0:T(8,128)S(1)} all-to-all(f32[8,48,128]{2,1,0:T(8,128)S(1)} %get-tuple-element.12), channel_id=1, replica_groups={{0,4,8,12,16,20,24,28},{1,5,9,13,17,21,25,29},{2,6,10,14,18,22,26,30},{..., dimensions={0} | all-to-all | bytes 393216 | tf_op jit(solution)/shard_map/all_to_all | solution.py:231
  64.0 0.7 far.1
  64.7 9.1 %all_to_all.26.sums = f32[16,16,128]{2,1,0:T(8,128)S(1)} all-to-all(f32[16,16,128]{2,1,0:T(8,128)S(1)} %get-tuple-element.14), channel_id=1, replica_groups=mesh['dp'=16,'ctx'=32] {'dp'}, dimensions={0} | all-to-all | bytes 262144 | tf_op jit(solution)/shard_map/all_to_all | solution.py:231
  73.8 17.4 %all_to_all.27.far = f32[8,24,128]{2,1,0:T(8,128)S(1)} all-to-all(f32[8,24,128]{2,1,0:T(8,128)S(1)} %sum.1), channel_id=1, replica_groups={{0,4,8,12,16,20,24,28},{1,5,9,13,17,21,25,29},{2,6,10,14,18,22,26,30},{..., dimensions={0} | all-to-all | bytes 196608 | tf_op jit(solution)/shard_map/all_to_all | solution.py:231
  91.2 1.4 %spread.1 = f32[4,192,128]{2,1,0:T(8,128)} custom-call(s32[2]{0:T(128)} %pad_add_fusion.place, f32[8,4096]{1,0:T(8,128)S(1)} %copy-done, f32[4,64,128]{2,1,0:T(8,128)S(1)} %get-tuple-element.11.carries, f32[8,24,128]{2,1,0:T(8,128)S(1)} %all_to_all.27.far), custom_call_target="tpu_custom_call" | custom-call | tf_op jit(solution)/shard_map/spread/pallas_call | solution.py:278
  92.6 3.5 %all-to-all-start.4 = ((f32[4,192,128]{2,1,0:T(8,128)}), f32[4,192,128]{2,1,0:T(8,128)S(1)}, u32[]{:S(2)}, u32[]{:S(2)}) async-start(f32[4,192,128]{2,1,0:T(8,128)} %spread.1), calls=%async_computation.4 | async-start | bytes 786432 | tf_op jit(solution)/shard_map/all_to_all | solution.py:231
  96.2 5.3 %inner.1 = f32[4096,128]{1,0:T(8,128)} custom-call(f32[4096,128]{1,0:T(8,128)} %get-tuple-element.9.grad, f32[8,4096]{1,0:T(8,128)} %decay.11, f32[8,4096]{1,0:T(8,128)} %residues.3), custom_call_target="tpu_custom_call" | custom-call | flops 16777216 | bytes 4194304 | tf_op jit(solution)/shard_map/inner/pallas_call | solution.py:234
  101.5 2.1 %all-to-all-done.4 = f32[4,192,128]{2,1,0:T(8,128)S(1)} async-done(((f32[4,192,128]{2,1,0:T(8,128)}), f32[4,192,128]{2,1,0:T(8,128)S(1)}, u32[]{:S(2)}, u32[]{:S(2)}) %all-to-all-start.4) | async-done | bytes 393248 | tf_op jit(solution)/shard_map/all_to_all | solution.py:231
  103.6 4.6 %final.1 = (bf16[1,128,4096]{2,1,0:T(8,128)(2,1)}, f32[8,4096]{1,0:T(8,128)}, f32[8,4096]{1,0:T(8,128)}) custom-call(f32[4096,128]{1,0:T(8,128)} %inner.1, f32[768,128]{1,0:T(8,128)S(1)} %bitcast.4, f32[8,4096]{1,0:T(8,128)} %decay.11, f32[8,4096]{1,0:T(8,128)} %residues.3), custom_call_target="tpu_custom_call" | custom-call | tf_op jit(solution)/shard_map/final/pallas_call | solution.py:288
  (1 shorter events, 0.0 us)
Async XLA Ops:
  0.6 30.2 %copy-start = (f32[8,4096]{1,0:T(8,128)S(1)}, f32[8,4096]{1,0:T(8,128)}, u32[]{:S(2)}) copy-start(f32[8,4096]{1,0:T(8,128)} %decay.11) | copy-start | bytes 393220
  12.7 18.1 %all-to-all-start = ((f32[4,384,128]{2,1,0:T(8,128)}), f32[4,384,128]{2,1,0:T(8,128)S(1)}, u32[]{:S(2)}, u32[]{:S(2)}) async-start(f32[4,384,128]{2,1,0:T(8,128)} %bitcast.2), calls=%async_computation | async-start | bytes 1572864 | tf_op jit(solution)/shard_map/all_to_all | solution.py:231
  92.6 10.9 %all-to-all-start.4 = ((f32[4,192,128]{2,1,0:T(8,128)}), f32[4,192,128]{2,1,0:T(8,128)S(1)}, u32[]{:S(2)}, u32[]{:S(2)}) async-start(f32[4,192,128]{2,1,0:T(8,128)} %spread.1), calls=%async_computation.4 | async-start | bytes 786432 | tf_op jit(solution)/shard_map/all_to_all | solution.py:231

commit v3 on v2

--- a/solution.py
+++ b/solution.py
@@ -16,6 +16,7 @@
 SENT = 6
 BACK = 3
 UNROLL = 4
+TILES = 4
 
 
 def rows(start, size):
@@ -27,43 +28,54 @@
         scratch[pl.ds(s, length, stride=SUBS), :] = read(slice(s * LANES, (s + 1) * LANES))
 
 
-def local_kernel(length, modes, values, gate, cotangent, decay, grad, sent, value_rows, decay_rows):
-    split_columns(lambda c: values[0, :, c].astype(F32), value_rows, length)
-    split_columns(
-        lambda c: cotangent[0, :, c].astype(F32) * gate[0, :, c].astype(F32), grad, length
-    )
-    split_columns(lambda c: decay[:, c], decay_rows, modes)
-    factor = [jnp.exp(-decay_rows[n * SUBS : (n + 1) * SUBS, :]) for n in range(modes)]
-    zero = [jnp.zeros((SUBS, LANES), F32)] * modes
-
-    def forward(t, carry):
-        state, moment, sum0, sum1 = (list(part) for part in carry)
-        value_now = value_rows[rows(t * SUBS, SUBS), :]
-        grad_now = grad[rows(t * SUBS, SUBS), :]
-        for n in range(modes):
-            moment[n] = factor[n] * (moment[n] + state[n])
-            state[n] = factor[n] * state[n] + value_now
-            sum0[n] = sum0[n] + grad_now * state[n]
-            sum1[n] = sum1[n] + grad_now * moment[n]
-        return state, moment, sum0, sum1
-
-    def backward(k, carry):
-        back, ramp = (list(part) for part in carry)
-        grad_now = grad[rows((length - 1 - k) * SUBS, SUBS), :]
-        for n in range(modes):
-            ramp[n] = factor[n] * (ramp[n] + back[n])
-            back[n] = factor[n] * back[n] + grad_now
-        return back, ramp
-
-    state, moment, sum0, sum1 = lax.fori_loop(
-        0, length, forward, (zero, zero, zero, zero), unroll=UNROLL
-    )
-    back, ramp = lax.fori_loop(0, length, backward, (zero, zero), unroll=UNROLL)
+def spread_row(ref, row):
+    return ref[pl.ds(row, SUBS, stride=0), :]
+
+
+def spread_cell(ref, row, columns):
+    return jnp.broadcast_to(ref[row : row + 1, columns], (SUBS, LANES))
+
+
+def local_kernel(length, modes, values, gate, cotangent, decay, grad, sent, value_rows, grad_rows):
     height = SENT * modes
-    first = pl.multiple_of(pl.program_id(0) * SUBS * height, SUBS * height)
-    for kind, part in enumerate((state, moment, back, ramp, sum0, sum1)):
-        for n in range(modes):
-            sent[pl.ds(first + kind * modes + n, SUBS, stride=height), :] = part[n]
+    step = pl.program_id(0)
+    for s in range(SUBS):
+        c, at = slice(s * LANES, (s + 1) * LANES), slice(s * length, (s + 1) * length)
+        value_rows[at, :] = values[0, :, c].astype(F32)
+        product = cotangent[0, :, c].astype(F32) * gate[0, :, c].astype(F32)
+        grad_rows[at, :] = product
+        grad[:, c] = product
+    zero = jnp.zeros((modes, LANES), F32)
+    for begin in range(0, SUBS, TILES):
+        columns = [slice((begin + i) * LANES, (begin + i + 1) * LANES) for i in range(TILES)]
+        factor = [jnp.exp(-decay[:, c]) for c in columns]
+
+        def advance(chunk, carry):
+            carry = [list(part) for part in carry]
+            early = pl.multiple_of(chunk * SUBS, SUBS)
+            late = pl.multiple_of(length - SUBS - chunk * SUBS, SUBS)
+            for j in range(SUBS):
+                for i in range(TILES):
+                    first = (begin + i) * length
+                    state, moment, back, ramp, sum0, sum1 = carry[i]
+                    value_now = spread_row(value_rows, first + early + j)
+                    grad_now = spread_row(grad_rows, first + early + j)
+                    moment = factor[i] * (moment + state)
+                    state = factor[i] * state + value_now
+                    sum0 = sum0 + grad_now * state
+                    sum1 = sum1 + grad_now * moment
+                    ramp = factor[i] * (ramp + back)
+                    back = factor[i] * back + spread_row(
+                        grad_rows, first + late + SUBS - 1 - j
+                    )
+                    carry[i] = [state, moment, back, ramp, sum0, sum1]
+            return carry
+
+        carry = lax.fori_loop(0, length // SUBS, advance, [[zero] * SENT for _ in columns])
+        for i, parts in enumerate(carry):
+            for kind, part in enumerate(parts):
+                at = (step * SUBS + begin + i) * height + kind * modes
+                sent[rows(at, modes), :] = part
 
 
 def joined(blocks, decay, span):
@@ -139,7 +151,16 @@
             arriving = fading * arriving
 
 
-def inner_kernel(length, modes, grad, decay, residues, total, decay_rows, residue_rows):
+def pairwise(terms):
+    while len(terms) > 1:
+        terms = [a + b for a, b in zip(terms[::2], terms[1::2])]
+    return terms[0]
+
+
+def inner_kernel(length, modes, grad, decay, residues, inner, grad_rows, total_rows, decay_rows,
+                 residue_rows):
+    step = pl.program_id(0)
+    split_columns(lambda c: grad[:, c], grad_rows, length)
     split_columns(lambda c: decay[:, c], decay_rows, modes)
     split_columns(lambda c: residues[:, c], residue_rows, modes)
     factor = [jnp.exp(-decay_rows[n * SUBS : (n + 1) * SUBS, :]) for n in range(modes)]
@@ -147,49 +168,47 @@
 
     def backward(k, back):
         at = rows((length - 1 - k) * SUBS, SUBS)
-        grad_now = grad[at, :]
+        grad_now = grad_rows[at, :]
         back = [factor[n] * back[n] + grad_now for n in range(modes)]
-        total[at, :] = pairwise([weight[n] * back[n] for n in range(modes)])
+        total_rows[at, :] = pairwise([weight[n] * back[n] for n in range(modes)])
         return back
 
     lax.fori_loop(
         0, length, backward, [jnp.zeros((SUBS, LANES), F32)] * modes, unroll=UNROLL
     )
-
-
-def pairwise(terms):
-    while len(terms) > 1:
-        terms = [a + b for a, b in zip(terms[::2], terms[1::2])]
-    return terms[0]
+    for s in range(SUBS):
+        to_inner = pl.ds(pl.multiple_of(step * WIDE + s * LANES, LANES), LANES)
+        inner[:, to_inner] = total_rows[pl.ds(s, length, stride=SUBS), :]
 
 
 def final_kernel(length, modes, scale, inner, arrived, decay, residues, input_grad, resid_grad,
-                 decay_grad, total_rows, decay_rows, residue_rows):
+                 decay_grad):
     height = BACK * modes
-    first = pl.multiple_of(pl.program_id(0) * SUBS * height, SUBS * height)
-    split_columns(lambda c: decay[:, c], decay_rows, modes)
-    split_columns(lambda c: residues[:, c], residue_rows, modes)
-    factor = [jnp.exp(-decay_rows[n * SUBS : (n + 1) * SUBS, :]) for n in range(modes)]
-    start = [
-        residue_rows[n * SUBS : (n + 1) * SUBS, :]
-        * arrived[pl.ds(first + n, SUBS, stride=height), :]
-        for n in range(modes)
-    ]
-
-    def backward(k, tail):
-        at = rows((length - 1 - k) * SUBS, SUBS)
-        tail = [factor[n] * tail[n] for n in range(modes)]
-        total_rows[at, :] = inner[at, :] + pairwise(tail)
-        return tail
-
-    lax.fori_loop(0, length, backward, start, unroll=UNROLL)
+    step = pl.program_id(0)
+    remaining = (
+        SUBS - lax.broadcasted_iota(jnp.int32, (SUBS, LANES), 0)
+    ).astype(F32)
     for s in range(SUBS):
-        cols = slice(s * LANES, (s + 1) * LANES)
-        input_grad[0, :, cols] = total_rows[pl.ds(s, length, stride=SUBS), :].astype(jnp.bfloat16)
-        at = first + s * height
-        resid_grad[:, cols] = arrived[rows(at + modes, modes), :] * scale
-        decay_grad[:, cols] = (
-            -decay[:, cols] * residues[:, cols] * arrived[rows(at + 2 * modes, modes), :] * scale
+        c = slice(s * LANES, (s + 1) * LANES)
+        from_inner = pl.ds(pl.multiple_of(step * WIDE + s * LANES, LANES), LANES)
+        at = (step * SUBS + s) * height
+        tail, chunk_factor = [], []
+        for n in range(modes):
+            rate = spread_cell(decay, n, c)
+            carry = spread_row(arrived, at + n)
+            tail.append(spread_cell(residues, n, c) * carry * jnp.exp(-rate * remaining))
+            chunk_factor.append(jnp.exp(-rate * float(SUBS)))
+        for low in range(length - 2 * SUBS, -1, -2 * SUBS):
+            pair = []
+            for begin in (low + SUBS, low):
+                pair.append(inner[begin : begin + SUBS, from_inner] + pairwise(tail))
+                tail = [f * z for f, z in zip(chunk_factor, tail)]
+            input_grad[0, low : low + 2 * SUBS, c] = jnp.concatenate(pair[::-1], 0).astype(
+                jnp.bfloat16
+            )
+        resid_grad[:, c] = arrived[rows(at + modes, modes), :] * scale
+        decay_grad[:, c] = (
+            -decay[:, c] * residues[:, c] * arrived[rows(at + 2 * modes, modes), :] * scale
         )
 
 
@@ -210,20 +229,18 @@
     on_chip = lambda x: pltpu.with_memory_space_constraint(x, pltpu.VMEM)
     held = lambda *dims: pltpu.VMEM(dims, F32)
 
+    small = pltpu.CompilerParams(vmem_limit_bytes=16 << 20)
     near_decay = on_chip(decay_rates)
     data = pl.BlockSpec((1, length, WIDE), lambda q: (0, 0, q))
+    block = pl.BlockSpec((length, WIDE), lambda q: (0, q))
     table = pl.BlockSpec((modes, WIDE), lambda q: (0, q))
-    flat = lambda size: pl.BlockSpec((size, LANES), lambda q: (q, 0))
     grad, sent = pl.pallas_call(
         functools.partial(local_kernel, length, modes),
         grid=(wide,),
         in_specs=[data, data, data, table],
-        out_specs=[flat(length * SUBS), vmem],
-        out_shape=[shape(wide * length * SUBS, LANES), held(wide * SUBS * SENT * modes, LANES)],
-        scratch_shapes=[
-            pltpu.VMEM((length * SUBS, LANES), F32),
-            pltpu.VMEM((modes * SUBS, LANES), F32),
-        ],
+        out_specs=[block, vmem],
+        out_shape=[shape(length, channels), held(wide * SUBS * SENT * modes, LANES)],
+        scratch_shapes=[pltpu.VMEM((SUBS * length, LANES), F32)] * 2,
         name="local",
     )(values, gate_values, cotangent, decay_rates)
 
@@ -234,18 +251,17 @@
     inner = pl.pallas_call(
         functools.partial(inner_kernel, length, modes),
         grid=(wide,),
-        in_specs=[flat(length * SUBS), table, table],
-        out_specs=flat(length * SUBS),
-        out_shape=shape(wide * length * SUBS, LANES),
-        scratch_shapes=[
-            pltpu.VMEM((modes * SUBS, LANES), F32),
-            pltpu.VMEM((modes * SUBS, LANES), F32),
-        ],
+        in_specs=[block, table, table],
+        out_specs=vmem,
+        out_shape=held(length, channels),
+        scratch_shapes=[pltpu.VMEM((length * SUBS, LANES), F32)] * 2
+        + [pltpu.VMEM((modes * SUBS, LANES), F32)] * 2,
         cost_estimate=pl.CostEstimate(
             flops=4 * modes * length * channels,
             bytes_accessed=8 * length * channels,
             transcendentals=0,
         ),
+        compiler_params=pltpu.CompilerParams(vmem_limit_bytes=60 << 20),
         name="inner",
     )(grad, decay_rates, residues)
     totals, near_carries = pl.pallas_call(
@@ -288,20 +304,16 @@
     return pl.pallas_call(
         functools.partial(final_kernel, length, modes, scale),
         grid=(wide,),
-        in_specs=[flat(length * SUBS), vmem, table, table],
+        in_specs=[vmem, vmem, table, table],
         out_specs=[data, table, table],
         out_shape=[
             jax.ShapeDtypeStruct(values.shape, jnp.bfloat16),
             shape(modes, channels),
             shape(modes, channels),
         ],
-        scratch_shapes=[
-            pltpu.VMEM((length * SUBS, LANES), F32),
-            pltpu.VMEM((modes * SUBS, LANES), F32),
-            pltpu.VMEM((modes * SUBS, LANES), F32),
-        ],
+        compiler_params=small,
         name="final",
-    )(inner, on_chip(arrived.reshape(-1, LANES)), decay_rates, residues)
+    )(on_chip(inner), on_chip(arrived.reshape(-1, LANES)), decay_rates, residues)
 
 
 def solution(mesh):

time: 110 us -> 106 us (0.964)
  Pallas kernels: 24.9 us -> 20.8 us
    pallas_call x1, Pallas kernels: 4.63 us -> 2.56 us  [on_device(): pl.pallas_call(functools.partial(final_kernel, length, modes, scale), gri...]
    pallas_call x1, Pallas kernels: 12.1 us -> 10.2 us  [on_device(): pl.pallas_call(functools.partial(local_kernel, length, modes), grid=(wide...]
where the time goes in v3:
time: 106 us; the launch traced here: 104 us
  blocking collectives  58.9 us (56%)
  Pallas kernels  20.8 us (20%)
  waiting for transfers between devices  13.9 us (13%)
  starting transfers between devices  9.35 us (9%)
    all_to_all x3, blocking collectives, exchange(): return lax.all_to_all(x, axis, 0, 0, tiled=True, axis_index_groups=groups)  58.9 us
    all_to_all x2, waiting for transfers between devices, exchange(): return lax.all_to_all(x, axis, 0, 0, tiled=True, axis_index_groups=groups)  13.9 us
    pallas_call x1, Pallas kernels, on_device(): pl.pallas_call(functools.partial(local_kernel, length, modes), grid=(wide...  10.2 us
    all_to_all x2, starting transfers between devices, exchange(): return lax.all_to_all(x, axis, 0, 0, tiled=True, axis_index_groups=groups)  9.35 us
    pallas_call x1, Pallas kernels, on_device(): pl.pallas_call(functools.partial(inner_kernel, length, modes), grid=(wide...  5.09 us
    pallas_call x1, Pallas kernels, on_device(): pl.pallas_call(functools.partial(final_kernel, length, modes, scale), gri...  2.56 us
  transfers between devices with their start and end apart: 2, of which 2 were waited for; matrix products, arithmetic and copies ran while one was open for 1% of the time, Pallas kernels for 5%

profile of v3, /device:TPU:6, one launch (start us, length us, event | category | flops | bytes accessed | tf_op | source)
XLA Modules:
  0.0 104.3 jit_solution(15634498602934769080)
XLA Ops:
  0.6 0.0 copy-start
  0.6 10.2 %local.1 = (f32[128,4096]{1,0:T(8,128)}, f32[1536,128]{1,0:T(8,128)}) custom-call(bf16[1,128,4096]{2,1,0:T(8,128)(2,1)} %values.1, bf16[1,128,4096]{2,1,0:T(8,128)(2,1)} %gate.1, bf16[1,128,4096]{2,1,0:T(8,128)(2,1)} %cotangent.1, f32[8,4096]{1,0:T(8,128)} %decay.11), custom_call_target="tpu_custom_call" | custom-call | tf_op jit(solution)/shard_map/local/pallas_call | solution.py:237
  10.9 5.8 %all-to-all-start = ((f32[4,384,128]{2,1,0:T(8,128)}), f32[4,384,128]{2,1,0:T(8,128)S(1)}, u32[]{:S(2)}, u32[]{:S(2)}) async-start(f32[4,384,128]{2,1,0:T(8,128)} %bitcast.2), calls=%async_computation | async-start | bytes 1572864 | tf_op jit(solution)/shard_map/all_to_all | solution.py:248
  16.7 0.6 pad_add_fusion.place
  17.3 11.6 %all-to-all-done.data = f32[4,384,128]{2,1,0:T(8,128)S(1)} async-done(((f32[4,384,128]{2,1,0:T(8,128)}), f32[4,384,128]{2,1,0:T(8,128)S(1)}, u32[]{:S(2)}, u32[]{:S(2)}) %all-to-all-start) | async-done | bytes 786464 | tf_op jit(solution)/shard_map/all_to_all | solution.py:248
  29.0 0.0 copy-done
  29.0 0.8 near.1
  29.7 32.4 %all_to_all.25.data = f32[8,48,128]{2,1,0:T(8,128)S(1)} all-to-all(f32[8,48,128]{2,1,0:T(8,128)S(1)} %get-tuple-element.12), channel_id=1, replica_groups={{0,4,8,12,16,20,24,28},{1,5,9,13,17,21,25,29},{2,6,10,14,18,22,26,30},{..., dimensions={0} | all-to-all | bytes 393216 | tf_op jit(solution)/shard_map/all_to_all | solution.py:248
  62.2 0.7 far.1
  62.9 9.1 %all_to_all.26.sums = f32[16,16,128]{2,1,0:T(8,128)S(1)} all-to-all(f32[16,16,128]{2,1,0:T(8,128)S(1)} %get-tuple-element.14), channel_id=1, replica_groups=mesh['dp'=16,'ctx'=32] {'dp'}, dimensions={0} | all-to-all | bytes 262144 | tf_op jit(solution)/shard_map/all_to_all | solution.py:248
  72.0 17.4 %all_to_all.27.far = f32[8,24,128]{2,1,0:T(8,128)S(1)} all-to-all(f32[8,24,128]{2,1,0:T(8,128)S(1)} %sum.1), channel_id=1, replica_groups={{0,4,8,12,16,20,24,28},{1,5,9,13,17,21,25,29},{2,6,10,14,18,22,26,30},{..., dimensions={0} | all-to-all | bytes 196608 | tf_op jit(solution)/shard_map/all_to_all | solution.py:248
  89.4 1.4 %spread.1 = f32[4,192,128]{2,1,0:T(8,128)} custom-call(s32[2]{0:T(128)} %pad_add_fusion.place, f32[8,4096]{1,0:T(8,128)S(1)} %copy-done, f32[4,64,128]{2,1,0:T(8,128)S(1)} %get-tuple-element.11.carries, f32[8,24,128]{2,1,0:T(8,128)S(1)} %all_to_all.27.far), custom_call_target="tpu_custom_call" | custom-call | tf_op jit(solution)/shard_map/spread/pallas_call | solution.py:294
  90.8 3.5 %all-to-all-start.4 = ((f32[4,192,128]{2,1,0:T(8,128)}), f32[4,192,128]{2,1,0:T(8,128)S(1)}, u32[]{:S(2)}, u32[]{:S(2)}) async-start(f32[4,192,128]{2,1,0:T(8,128)} %spread.1), calls=%async_computation.4 | async-start | bytes 786432 | tf_op jit(solution)/shard_map/all_to_all | solution.py:248
  94.3 0.0 copy-start.1
  94.3 0.0 copy-start.2
  94.3 5.1 %inner.1 = f32[128,4096]{1,0:T(8,128)S(1)} custom-call(f32[128,4096]{1,0:T(8,128)} %get-tuple-element.9.grad, f32[8,4096]{1,0:T(8,128)} %decay.11, f32[8,4096]{1,0:T(8,128)} %residues.3), custom_call_target="tpu_custom_call" | custom-call | flops 16777216 | bytes 4194304 | tf_op jit(solution)/shard_map/inner/pallas_call | solution.py:251
  99.4 2.3 %all-to-all-done.4 = f32[4,192,128]{2,1,0:T(8,128)S(1)} async-done(((f32[4,192,128]{2,1,0:T(8,128)}), f32[4,192,128]{2,1,0:T(8,128)S(1)}, u32[]{:S(2)}, u32[]{:S(2)}) %all-to-all-start.4) | async-done | bytes 393248 | tf_op jit(solution)/shard_map/all_to_all | solution.py:248
  101.7 0.0 copy-done.1
  101.7 0.0 copy-done.2
  101.7 2.6 %final.1 = (bf16[1,128,4096]{2,1,0:T(8,128)(2,1)}, f32[8,4096]{1,0:T(8,128)}, f32[8,4096]{1,0:T(8,128)}) custom-call(f32[128,4096]{1,0:T(8,128)S(1)} %inner.1, f32[768,128]{1,0:T(8,128)S(1)} %bitcast.4, f32[8,4096]{1,0:T(8,128)S(1)} %copy-done.1, f32[8,4096]{1,0:T(8,128)S(1)} %copy-done.2), custom_call_target="tpu_custom_call" | custom-call | tf_op jit(solution)/shard_map/final/pallas_call | solution.py:304
  (1 shorter events, 0.0 us)
Async XLA Ops:
  0.6 28.3 %copy-start = (f32[8,4096]{1,0:T(8,128)S(1)}, f32[8,4096]{1,0:T(8,128)}, u32[]{:S(2)}) copy-start(f32[8,4096]{1,0:T(8,128)} %decay.11) | copy-start | bytes 393220
  10.9 18.1 %all-to-all-start = ((f32[4,384,128]{2,1,0:T(8,128)}), f32[4,384,128]{2,1,0:T(8,128)S(1)}, u32[]{:S(2)}, u32[]{:S(2)}) async-start(f32[4,384,128]{2,1,0:T(8,128)} %bitcast.2), calls=%async_computation | async-start | bytes 1572864 | tf_op jit(solution)/shard_map/all_to_all | solution.py:248
  90.8 10.9 %all-to-all-start.4 = ((f32[4,192,128]{2,1,0:T(8,128)}), f32[4,192,128]{2,1,0:T(8,128)S(1)}, u32[]{:S(2)}, u32[]{:S(2)}) async-start(f32[4,192,128]{2,1,0:T(8,128)} %spread.1), calls=%async_computation.4 | async-start | bytes 786432 | tf_op jit(solution)/shard_map/all_to_all | solution.py:248
  94.3 7.4 %copy-start.1 = (f32[8,4096]{1,0:T(8,128)S(1)}, f32[8,4096]{1,0:T(8,128)}, u32[]{:S(2)}) copy-start(f32[8,4096]{1,0:T(8,128)} %decay.11) | copy-start | bytes 393220
  94.3 7.4 %copy-start.2 = (f32[8,4096]{1,0:T(8,128)S(1)}, f32[8,4096]{1,0:T(8,128)}, u32[]{:S(2)}) copy-start(f32[8,4096]{1,0:T(8,128)} %residues.3) | copy-start | bytes 393220

commit v4 on v3

--- a/solution.py
+++ b/solution.py
@@ -36,15 +36,13 @@
     return jnp.broadcast_to(ref[row : row + 1, columns], (SUBS, LANES))
 
 
-def local_kernel(length, modes, values, gate, cotangent, decay, grad, sent, value_rows, grad_rows):
+def local_kernel(length, modes, values, gate, cotangent, decay, sent, value_rows, grad_rows):
     height = SENT * modes
     step = pl.program_id(0)
     for s in range(SUBS):
         c, at = slice(s * LANES, (s + 1) * LANES), slice(s * length, (s + 1) * length)
         value_rows[at, :] = values[0, :, c].astype(F32)
-        product = cotangent[0, :, c].astype(F32) * gate[0, :, c].astype(F32)
-        grad_rows[at, :] = product
-        grad[:, c] = product
+        grad_rows[at, :] = cotangent[0, :, c].astype(F32) * gate[0, :, c].astype(F32)
     zero = jnp.zeros((modes, LANES), F32)
     for begin in range(0, SUBS, TILES):
         columns = [slice((begin + i) * LANES, (begin + i + 1) * LANES) for i in range(TILES)]
@@ -157,10 +155,12 @@
     return terms[0]
 
 
-def inner_kernel(length, modes, grad, decay, residues, inner, grad_rows, total_rows, decay_rows,
-                 residue_rows):
+def inner_kernel(length, modes, gate, cotangent, decay, residues, inner, grad_rows, total_rows,
+                 decay_rows, residue_rows):
     step = pl.program_id(0)
-    split_columns(lambda c: grad[:, c], grad_rows, length)
+    split_columns(
+        lambda c: cotangent[0, :, c].astype(F32) * gate[0, :, c].astype(F32), grad_rows, length
+    )
     split_columns(lambda c: decay[:, c], decay_rows, modes)
     split_columns(lambda c: residues[:, c], residue_rows, modes)
     factor = [jnp.exp(-decay_rows[n * SUBS : (n + 1) * SUBS, :]) for n in range(modes)]
@@ -221,6 +221,7 @@
     assert modes == SUBS and wide == NEAR and far == SUBS and values.shape[0] == 1
     me = lax.axis_index("ctx")
     place = jnp.stack([me % NEAR, (me % NEAR) * SUBS + me // NEAR]).astype(jnp.int32)
+    place, values = lax.optimization_barrier((place, values))
     near_groups = [[g * NEAR + k for k in range(NEAR)] for g in range(far)]
     far_groups = [[k * NEAR + g for k in range(far)] for g in range(NEAR)]
     shape = lambda *dims: jax.ShapeDtypeStruct(dims, F32)
@@ -232,14 +233,13 @@
     small = pltpu.CompilerParams(vmem_limit_bytes=16 << 20)
     near_decay = on_chip(decay_rates)
     data = pl.BlockSpec((1, length, WIDE), lambda q: (0, 0, q))
-    block = pl.BlockSpec((length, WIDE), lambda q: (0, q))
     table = pl.BlockSpec((modes, WIDE), lambda q: (0, q))
-    grad, sent = pl.pallas_call(
+    sent = pl.pallas_call(
         functools.partial(local_kernel, length, modes),
         grid=(wide,),
         in_specs=[data, data, data, table],
-        out_specs=[block, vmem],
-        out_shape=[shape(length, channels), held(wide * SUBS * SENT * modes, LANES)],
+        out_specs=vmem,
+        out_shape=held(wide * SUBS * SENT * modes, LANES),
         scratch_shapes=[pltpu.VMEM((SUBS * length, LANES), F32)] * 2,
         name="local",
     )(values, gate_values, cotangent, decay_rates)
@@ -251,7 +251,7 @@
     inner = pl.pallas_call(
         functools.partial(inner_kernel, length, modes),
         grid=(wide,),
-        in_specs=[block, table, table],
+        in_specs=[data, data, table, table],
         out_specs=vmem,
         out_shape=held(length, channels),
         scratch_shapes=[pltpu.VMEM((length * SUBS, LANES), F32)] * 2
@@ -263,7 +263,7 @@
         ),
         compiler_params=pltpu.CompilerParams(vmem_limit_bytes=60 << 20),
         name="inner",
-    )(grad, decay_rates, residues)
+    )(gate_values, cotangent, decay_rates, residues)
     totals, near_carries = pl.pallas_call(
         functools.partial(near_kernel, float(length), modes),
         in_specs=[smem, vmem, vmem],

time: 106 us -> 105 us (level)
  blocking collectives: 58.9 us -> 76.4 us
  waiting for transfers between devices: 13.9 us -> 1.85 us
  starting transfers between devices: 9.35 us -> 3.46 us
    all_to_all x3 -> x4, blocking collectives: 58.9 us -> 76.4 us  [exchange(): return lax.all_to_all(x, axis, 0, 0, tiled=True, axis_index_groups=groups)]
    all_to_all x2 -> x1, waiting for transfers between devices: 13.9 us -> 1.85 us  [exchange(): return lax.all_to_all(x, axis, 0, 0, tiled=True, axis_index_groups=groups)]
    all_to_all x2 -> x1, starting transfers between devices: 9.35 us -> 3.46 us  [exchange(): return lax.all_to_all(x, axis, 0, 0, tiled=True, axis_index_groups=groups)]
    pallas_call x1, Pallas kernels: 10.2 us -> 8.96 us  [on_device(): pl.pallas_call(functools.partial(local_kernel, length, modes), grid=(wide...]
  transfers between devices with their start and end apart: 2 -> 1, of which waited for: 2 -> 1; matrix products, arithmetic and copies ran while one was open for 1% -> 0% of each run, Pallas kernels for 5% -> 5%
where the time goes in v4:
time: 105 us; the launch traced here: 103 us
  blocking collectives  76.4 us (73%)
  Pallas kernels  19.9 us (19%)
  starting transfers between devices  3.46 us (3%)
  waiting for transfers between devices  1.85 us (2%)
    all_to_all x4, blocking collectives, exchange(): return lax.all_to_all(x, axis, 0, 0, tiled=True, axis_index_groups=groups)  76.4 us
    pallas_call x1, Pallas kernels, on_device(): pl.pallas_call(functools.partial(local_kernel, length, modes), grid=(wide...  8.96 us
    pallas_call x1, Pallas kernels, on_device(): pl.pallas_call(functools.partial(inner_kernel, length, modes), grid=(wide...  5.46 us
    all_to_all x1, starting transfers between devices, exchange(): return lax.all_to_all(x, axis, 0, 0, tiled=True, axis_index_groups=groups)  3.46 us
    pallas_call x1, Pallas kernels, on_device(): pl.pallas_call(functools.partial(final_kernel, length, modes, scale), gri...  2.56 us
  transfers between devices with their start and end apart: 1, of which 1 were waited for; matrix products, arithmetic and copies ran while one was open for 0% of the time, Pallas kernels for 5%

profile of v4, /device:TPU:6, one launch (start us, length us, event | category | flops | bytes accessed | tf_op | source)
XLA Modules:
  0.0 103.0 jit_solution(5129719974540998074)
XLA Ops:
  0.7 0.7 pad_add_fusion.place
  1.3 0.0 copy-start
  1.3 9.0 %local.1 = f32[1536,128]{1,0:T(8,128)S(1)} custom-call(bf16[1,128,4096]{2,1,0:T(8,128)(2,1)} %values, bf16[1,128,4096]{2,1,0:T(8,128)(2,1)} %gate.3, bf16[1,128,4096]{2,1,0:T(8,128)(2,1)} %cotangent.3, f32[8,4096]{1,0:T(8,128)} %decay.11), custom_call_target="tpu_custom_call" | custom-call | tf_op jit(solution)/shard_map/local/pallas_call | solution.py:237
  10.3 18.5 %all_to_all.25.data = f32[4,384,128]{2,1,0:T(8,128)S(1)} all-to-all(f32[4,384,128]{2,1,0:T(8,128)S(1)} %bitcast.4), channel_id=1, replica_groups={{0,1,2,3},{4,5,6,7},{8,9,10,11},{12,13,14,15},{16,17,18,19},{20,21,22,2..., dimensions={0} | all-to-all | bytes 1572864 | tf_op jit(solution)/shard_map/all_to_all | solution.py:248
  28.7 0.0 copy-done
  28.7 0.8 near.1
  29.5 31.0 %all_to_all.26.data = f32[8,48,128]{2,1,0:T(8,128)S(1)} all-to-all(f32[8,48,128]{2,1,0:T(8,128)S(1)} %get-tuple-element.12), channel_id=1, replica_groups={{0,4,8,12,16,20,24,28},{1,5,9,13,17,21,25,29},{2,6,10,14,18,22,26,30},{..., dimensions={0} | all-to-all | bytes 393216 | tf_op jit(solution)/shard_map/all_to_all | solution.py:248
  60.5 0.7 far.1
  61.3 9.1 %all_to_all.27.sums = f32[16,16,128]{2,1,0:T(8,128)S(1)} all-to-all(f32[16,16,128]{2,1,0:T(8,128)S(1)} %get-tuple-element.14), channel_id=1, replica_groups=mesh['dp'=16,'ctx'=32] {'dp'}, dimensions={0} | all-to-all | bytes 262144 | tf_op jit(solution)/shard_map/all_to_all | solution.py:248
  70.3 17.8 %all_to_all.28.far = f32[8,24,128]{2,1,0:T(8,128)S(1)} all-to-all(f32[8,24,128]{2,1,0:T(8,128)S(1)} %sum.1), channel_id=1, replica_groups={{0,4,8,12,16,20,24,28},{1,5,9,13,17,21,25,29},{2,6,10,14,18,22,26,30},{..., dimensions={0} | all-to-all | bytes 196608 | tf_op jit(solution)/shard_map/all_to_all | solution.py:248
  88.2 1.4 %spread.1 = f32[4,192,128]{2,1,0:T(8,128)} custom-call(s32[2]{0:T(128)} %pad_add_fusion.place, f32[8,4096]{1,0:T(8,128)S(1)} %copy-done, f32[4,64,128]{2,1,0:T(8,128)S(1)} %get-tuple-element.11.carries, f32[8,24,128]{2,1,0:T(8,128)S(1)} %all_to_all.28.far), custom_call_target="tpu_custom_call" | custom-call | tf_op jit(solution)/shard_map/spread/pallas_call | solution.py:294
  89.6 3.5 %all-to-all-start.4 = ((f32[4,192,128]{2,1,0:T(8,128)}), f32[4,192,128]{2,1,0:T(8,128)S(1)}, u32[]{:S(2)}, u32[]{:S(2)}) async-start(f32[4,192,128]{2,1,0:T(8,128)} %spread.1), calls=%async_computation.4 | async-start | bytes 786432 | tf_op jit(solution)/shard_map/all_to_all | solution.py:248
  93.1 0.0 copy-start.1
  93.1 0.0 copy-start.2
  93.1 5.5 %inner.1 = f32[128,4096]{1,0:T(8,128)S(1)} custom-call(bf16[1,128,4096]{2,1,0:T(8,128)(2,1)} %gate.3, bf16[1,128,4096]{2,1,0:T(8,128)(2,1)} %cotangent.3, f32[8,4096]{1,0:T(8,128)} %decay.11, f32[8,4096]{1,0:T(8,128)} %residues.3), custom_call_target="tpu_custom_call" | custom-call | flops 16777216 | bytes 4194304 | tf_op jit(solution)/shard_map/inner/pallas_call | solution.py:251
  98.6 1.8 %all-to-all-done.4 = f32[4,192,128]{2,1,0:T(8,128)S(1)} async-done(((f32[4,192,128]{2,1,0:T(8,128)}), f32[4,192,128]{2,1,0:T(8,128)S(1)}, u32[]{:S(2)}, u32[]{:S(2)}) %all-to-all-start.4) | async-done | bytes 393248 | tf_op jit(solution)/shard_map/all_to_all | solution.py:248
  100.4 0.0 copy-done.1
  100.4 0.0 copy-done.2
  100.4 2.6 %final.1 = (bf16[1,128,4096]{2,1,0:T(8,128)(2,1)}, f32[8,4096]{1,0:T(8,128)}, f32[8,4096]{1,0:T(8,128)}) custom-call(f32[128,4096]{1,0:T(8,128)S(1)} %inner.1, f32[768,128]{1,0:T(8,128)S(1)} %bitcast.5, f32[8,4096]{1,0:T(8,128)S(1)} %copy-done.1, f32[8,4096]{1,0:T(8,128)S(1)} %copy-done.2), custom_call_target="tpu_custom_call" | custom-call | tf_op jit(solution)/shard_map/final/pallas_call | solution.py:304
  (1 shorter events, 0.0 us)
Async XLA Ops:
  1.3 27.4 %copy-start = (f32[8,4096]{1,0:T(8,128)S(1)}, f32[8,4096]{1,0:T(8,128)}, u32[]{:S(2)}) copy-start(f32[8,4096]{1,0:T(8,128)} %decay.11) | copy-start | bytes 393220
  89.6 10.8 %all-to-all-start.4 = ((f32[4,192,128]{2,1,0:T(8,128)}), f32[4,192,128]{2,1,0:T(8,128)S(1)}, u32[]{:S(2)}, u32[]{:S(2)}) async-start(f32[4,192,128]{2,1,0:T(8,128)} %spread.1), calls=%async_computation.4 | async-start | bytes 786432 | tf_op jit(solution)/shard_map/all_to_all | solution.py:248
  93.1 7.3 %copy-start.1 = (f32[8,4096]{1,0:T(8,128)S(1)}, f32[8,4096]{1,0:T(8,128)}, u32[]{:S(2)}) copy-start(f32[8,4096]{1,0:T(8,128)} %decay.11) | copy-start | bytes 393220
  93.1 7.3 %copy-start.2 = (f32[8,4096]{1,0:T(8,128)S(1)}, f32[8,4096]{1,0:T(8,128)}, u32[]{:S(2)}) copy-start(f32[8,4096]{1,0:T(8,128)} %residues.3) | copy-start | bytes 393220

commit v5 on v4

--- a/solution.py
+++ b/solution.py
@@ -16,6 +16,7 @@
 SENT = 6
 BACK = 3
 UNROLL = 4
+FINAL = 2
 TILES = 4
 
 
@@ -188,10 +189,11 @@
     remaining = (
         SUBS - lax.broadcasted_iota(jnp.int32, (SUBS, LANES), 0)
     ).astype(F32)
-    for s in range(SUBS):
+    tiles = decay.shape[1] // LANES
+    for s in range(tiles):
         c = slice(s * LANES, (s + 1) * LANES)
-        from_inner = pl.ds(pl.multiple_of(step * WIDE + s * LANES, LANES), LANES)
-        at = (step * SUBS + s) * height
+        from_inner = pl.ds(pl.multiple_of((step * tiles + s) * LANES, LANES), LANES)
+        at = (step * tiles + s) * height
         tail, chunk_factor = [], []
         for n in range(modes):
             rate = spread_cell(decay, n, c)
@@ -230,6 +232,7 @@
     on_chip = lambda x: pltpu.with_memory_space_constraint(x, pltpu.VMEM)
     held = lambda *dims: pltpu.VMEM(dims, F32)
 
+    part = pl.BlockSpec((modes, channels // FINAL), lambda q: (0, q))
     small = pltpu.CompilerParams(vmem_limit_bytes=16 << 20)
     near_decay = on_chip(decay_rates)
     data = pl.BlockSpec((1, length, WIDE), lambda q: (0, 0, q))
@@ -273,6 +276,7 @@
     )(place, near_decay, on_chip(near_data))
 
     far_data = exchange(totals, "ctx", far_groups)
+    far_data, inner = lax.optimization_barrier((far_data, inner))
     far_carries, sums = pl.pallas_call(
         functools.partial(far_kernel, float(length * NEAR), modes),
         in_specs=[smem, vmem, vmem],
@@ -303,9 +307,9 @@
     scale = 1.0 / math.sqrt(rows_of * length * peers)
     return pl.pallas_call(
         functools.partial(final_kernel, length, modes, scale),
-        grid=(wide,),
-        in_specs=[vmem, vmem, table, table],
-        out_specs=[data, table, table],
+        grid=(FINAL,),
+        in_specs=[vmem, vmem, part, part],
+        out_specs=[pl.BlockSpec((1, length, channels // FINAL), lambda q: (0, 0, q)), part, part],
         out_shape=[
             jax.ShapeDtypeStruct(values.shape, jnp.bfloat16),
             shape(modes, channels),

time: 105 us -> 104 us (level)
  blocking collectives: 76.4 us -> 56 us
  starting transfers between devices: 3.46 us -> 14.2 us
  waiting for transfers between devices: 1.85 us -> 11.6 us
    all_to_all x4, blocking collectives: 76.4 us -> 56 us  [exchange(): return lax.all_to_all(x, axis, 0, 0, tiled=True, axis_index_groups=groups)]
    all_to_all x1, starting transfers between devices: 3.46 us -> 14.2 us  [exchange(): return lax.all_to_all(x, axis, 0, 0, tiled=True, axis_index_groups=groups)]
    all_to_all x1, waiting for transfers between devices: 1.85 us -> 11.6 us  [exchange(): return lax.all_to_all(x, axis, 0, 0, tiled=True, axis_index_groups=groups)]
where the time goes in v5:
time: 104 us; the launch traced here: 103 us
  blocking collectives  56 us (54%)
  Pallas kernels  19.5 us (19%)
  starting transfers between devices  14.2 us (14%)
  waiting for transfers between devices  11.6 us (11%)
    all_to_all x4, blocking collectives, exchange(): return lax.all_to_all(x, axis, 0, 0, tiled=True, axis_index_groups=groups)  56 us
    all_to_all x1, starting transfers between devices, exchange(): return lax.all_to_all(x, axis, 0, 0, tiled=True, axis_index_groups=groups)  14.2 us
    all_to_all x1, waiting for transfers between devices, exchange(): return lax.all_to_all(x, axis, 0, 0, tiled=True, axis_index_groups=groups)  11.6 us
    pallas_call x1, Pallas kernels, on_device(): pl.pallas_call(functools.partial(local_kernel, length, modes), grid=(wide...  8.96 us
    pallas_call x1, Pallas kernels, on_device(): pl.pallas_call(functools.partial(inner_kernel, length, modes), grid=(wide...  5.42 us
    pallas_call x1, Pallas kernels, on_device(): pl.pallas_call(functools.partial(final_kernel, length, modes, scale), gri...  2.28 us
  transfers between devices with their start and end apart: 1, of which 1 were waited for; matrix products, arithmetic and copies ran while one was open for 0% of the time, Pallas kernels for 5%

profile of v5, /device:TPU:6, one launch (start us, length us, event | category | flops | bytes accessed | tf_op | source)
XLA Modules:
  0.0 102.7 jit_solution(13883324193825919702)
XLA Ops:
  0.7 0.7 pad_add_fusion.place
  1.3 0.0 copy-start
  1.3 9.0 %local.1 = f32[1536,128]{1,0:T(8,128)S(1)} custom-call(bf16[1,128,4096]{2,1,0:T(8,128)(2,1)} %values, bf16[1,128,4096]{2,1,0:T(8,128)(2,1)} %gate.3, bf16[1,128,4096]{2,1,0:T(8,128)(2,1)} %cotangent.3, f32[8,4096]{1,0:T(8,128)} %decay.11), custom_call_target="tpu_custom_call" | custom-call | tf_op jit(solution)/shard_map/local/pallas_call | solution.py:240
  10.3 18.5 %all_to_all.25.data = f32[4,384,128]{2,1,0:T(8,128)S(1)} all-to-all(f32[4,384,128]{2,1,0:T(8,128)S(1)} %bitcast.4), channel_id=1, replica_groups={{0,1,2,3},{4,5,6,7},{8,9,10,11},{12,13,14,15},{16,17,18,19},{20,21,22,2..., dimensions={0} | all-to-all | bytes 1572864 | tf_op jit(solution)/shard_map/all_to_all | solution.py:251
  28.7 0.0 copy-done
  28.7 1.5 %near.1 = (f32[8,48,128]{2,1,0:T(8,128)}, f32[4,64,128]{2,1,0:T(8,128)S(1)}) custom-call(s32[2]{0:T(128)} %pad_add_fusion.place, f32[8,4096]{1,0:T(8,128)S(1)} %copy-done, f32[4,384,128]{2,1,0:T(8,128)S(1)} %all_to_all.25.data), custom_call_target="tpu_custom_call" | custom-call | tf_op jit(solution)/shard_map/near/pallas_call | solution.py:270
  30.2 14.2 %all-to-all-start.1 = ((f32[8,48,128]{2,1,0:T(8,128)}), f32[8,48,128]{2,1,0:T(8,128)S(1)}, u32[]{:S(2)}, u32[]{:S(2)}) async-start(f32[8,48,128]{2,1,0:T(8,128)} %get-tuple-element.13), calls=%async_computation.1 | async-start | bytes 393216 | tf_op jit(solution)/shard_map/all_to_all | solution.py:251
  44.4 0.0 copy-start.1
  44.4 5.4 %inner.1 = f32[128,4096]{1,0:T(8,128)S(1)} custom-call(bf16[1,128,4096]{2,1,0:T(8,128)(2,1)} %gate.3, bf16[1,128,4096]{2,1,0:T(8,128)(2,1)} %cotangent.3, f32[8,4096]{1,0:T(8,128)} %decay.11, f32[8,4096]{1,0:T(8,128)} %residues.3), custom_call_target="tpu_custom_call" | custom-call | flops 16777216 | bytes 4194304 | tf_op jit(solution)/shard_map/inner/pallas_call | solution.py:254
  49.8 0.0 copy-start.2
  49.8 11.6 %all-to-all-done.1.data = f32[8,48,128]{2,1,0:T(8,128)S(1)} async-done(((f32[8,48,128]{2,1,0:T(8,128)}), f32[8,48,128]{2,1,0:T(8,128)S(1)}, u32[]{:S(2)}, u32[]{:S(2)}) %all-to-all-start.1) | async-done | bytes 196640 | tf_op jit(solution)/shard_map/all_to_all | solution.py:251
  61.4 0.0 copy-done.1
  61.4 0.7 far.1
  62.1 9.1 %all_to_all.26.sums = f32[16,16,128]{2,1,0:T(8,128)S(1)} all-to-all(f32[16,16,128]{2,1,0:T(8,128)S(1)} %get-tuple-element.18), channel_id=1, replica_groups=mesh['dp'=16,'ctx'=32] {'dp'}, dimensions={0} | all-to-all | bytes 262144 | tf_op jit(solution)/shard_map/all_to_all | solution.py:251
  71.2 17.8 %all_to_all.27.far = f32[8,24,128]{2,1,0:T(8,128)S(1)} all-to-all(f32[8,24,128]{2,1,0:T(8,128)S(1)} %sum.1), channel_id=1, replica_groups={{0,4,8,12,16,20,24,28},{1,5,9,13,17,21,25,29},{2,6,10,14,18,22,26,30},{..., dimensions={0} | all-to-all | bytes 196608 | tf_op jit(solution)/shard_map/all_to_all | solution.py:251
  89.0 0.7 spread.1
  89.7 10.6 %all_to_all.28 = f32[4,192,128]{2,1,0:T(8,128)S(1)} all-to-all(f32[4,192,128]{2,1,0:T(8,128)S(1)} %spread.1), channel_id=1, replica_groups={{0,1,2,3},{4,5,6,7},{8,9,10,11},{12,13,14,15},{16,17,18,19},{20,21,22,2..., dimensions={0} | all-to-all | bytes 786432 | tf_op jit(solution)/shard_map/all_to_all | solution.py:251
  100.4 0.0 copy-done.2
  100.4 2.3 %final.1 = (bf16[1,128,4096]{2,1,0:T(8,128)(2,1)}, f32[8,4096]{1,0:T(8,128)}, f32[8,4096]{1,0:T(8,128)}) custom-call(f32[128,4096]{1,0:T(8,128)S(1)} %inner.1, f32[768,128]{1,0:T(8,128)S(1)} %bitcast.5, f32[8,4096]{1,0:T(8,128)S(1)} %copy-done.1, f32[8,4096]{1,0:T(8,128)S(1)} %copy-done.2), custom_call_target="tpu_custom_call" | custom-call | tf_op jit(solution)/shard_map/final/pallas_call | solution.py:308
  (1 shorter events, 0.0 us)
Async XLA Ops:
  1.3 27.4 %copy-start = (f32[8,4096]{1,0:T(8,128)S(1)}, f32[8,4096]{1,0:T(8,128)}, u32[]{:S(2)}) copy-start(f32[8,4096]{1,0:T(8,128)} %decay.11) | copy-start | bytes 393220
  30.2 31.2 %all-to-all-start.1 = ((f32[8,48,128]{2,1,0:T(8,128)}), f32[8,48,128]{2,1,0:T(8,128)S(1)}, u32[]{:S(2)}, u32[]{:S(2)}) async-start(f32[8,48,128]{2,1,0:T(8,128)} %get-tuple-element.13), calls=%async_computation.1 | async-start | bytes 393216 | tf_op jit(solution)/shard_map/all_to_all | solution.py:251
  44.4 17.0 %copy-start.1 = (f32[8,4096]{1,0:T(8,128)S(1)}, f32[8,4096]{1,0:T(8,128)}, u32[]{:S(2)}) copy-start(f32[8,4096]{1,0:T(8,128)} %decay.11) | copy-start | bytes 393220
  49.8 50.6 %copy-start.2 = (f32[8,4096]{1,0:T(8,128)S(1)}, f32[8,4096]{1,0:T(8,128)}, u32[]{:S(2)}) copy-start(f32[8,4096]{1,0:T(8,128)} %residues.3) | copy-start | bytes 393220

commit v6 on v5

--- a/solution.py
+++ b/solution.py
@@ -15,7 +15,7 @@
 NEAR = 4
 SENT = 6
 BACK = 3
-UNROLL = 4
+UNROLL = 8
 FINAL = 2
 TILES = 4
 
@@ -70,7 +70,7 @@
                     carry[i] = [state, moment, back, ramp, sum0, sum1]
             return carry
 
-        carry = lax.fori_loop(0, length // SUBS, advance, [[zero] * SENT for _ in columns])
+        carry = lax.fori_loop(0, length // SUBS, advance, [[zero] * SENT for _ in columns], unroll=4)
         for i, parts in enumerate(carry):
             for kind, part in enumerate(parts):
                 at = (step * SUBS + begin + i) * height + kind * modes
@@ -276,7 +276,6 @@
     )(place, near_decay, on_chip(near_data))
 
     far_data = exchange(totals, "ctx", far_groups)
-    far_data, inner = lax.optimization_barrier((far_data, inner))
     far_carries, sums = pl.pallas_call(
         functools.partial(far_kernel, float(length * NEAR), modes),
         in_specs=[smem, vmem, vmem],
@@ -295,6 +294,7 @@
     )(on_chip(far_carries), on_chip(all_sums))
 
     far_back = exchange(far_out, "ctx", far_groups)
+    far_back, inner = lax.optimization_barrier((far_back, inner))
     near_out = pl.pallas_call(
         functools.partial(spread_kernel, float(length), modes),
         in_specs=[smem, vmem, vmem, vmem],

time: 104 us -> 104 us (level)
  blocking collectives: 56 us -> 69.7 us
  starting transfers between devices: 14.2 us -> 3.36 us
  waiting for transfers between devices: 11.6 us -> 9.45 us
    all_to_all x4, blocking collectives: 56 us -> 69.7 us  [exchange(): return lax.all_to_all(x, axis, 0, 0, tiled=True, axis_index_groups=groups)]
    all_to_all x1, starting transfers between devices: 14.2 us -> 3.36 us  [exchange(): return lax.all_to_all(x, axis, 0, 0, tiled=True, axis_index_groups=groups)]
    all_to_all x1, waiting for transfers between devices: 11.6 us -> 9.45 us  [exchange(): return lax.all_to_all(x, axis, 0, 0, tiled=True, axis_index_groups=groups)]
where the time goes in v6:
time: 104 us; the launch traced here: 103 us
  blocking collectives  69.7 us (67%)
  Pallas kernels  18.8 us (18%)
  waiting for transfers between devices  9.45 us (9%)
  starting transfers between devices  3.36 us (3%)
    all_to_all x4, blocking collectives, exchange(): return lax.all_to_all(x, axis, 0, 0, tiled=True, axis_index_groups=groups)  69.7 us
    all_to_all x1, waiting for transfers between devices, exchange(): return lax.all_to_all(x, axis, 0, 0, tiled=True, axis_index_groups=groups)  9.45 us
    pallas_call x1, Pallas kernels, on_device(): pl.pallas_call(functools.partial(local_kernel, length, modes), grid=(wide...  8.47 us
    pallas_call x1, Pallas kernels, on_device(): pl.pallas_call(functools.partial(inner_kernel, length, modes), grid=(wide...  5.26 us
    all_to_all x1, starting transfers between devices, exchange(): return lax.all_to_all(x, axis, 0, 0, tiled=True, axis_index_groups=groups)  3.36 us
    pallas_call x1, Pallas kernels, on_device(): pl.pallas_call(functools.partial(final_kernel, length, modes, scale), gri...  2.28 us
  transfers between devices with their start and end apart: 1, of which 1 were waited for; matrix products, arithmetic and copies ran while one was open for 0% of the time, Pallas kernels for 5%

profile of v6, /device:TPU:6, one launch (start us, length us, event | category | flops | bytes accessed | tf_op | source)
XLA Modules:
  0.0 102.6 jit_solution(16092589960362405901)
XLA Ops:
  0.7 0.6 pad_add_fusion.place
  1.2 0.0 copy-start
  1.2 8.5 %local.1 = f32[1536,128]{1,0:T(8,128)S(1)} custom-call(bf16[1,128,4096]{2,1,0:T(8,128)(2,1)} %values, bf16[1,128,4096]{2,1,0:T(8,128)(2,1)} %gate.3, bf16[1,128,4096]{2,1,0:T(8,128)(2,1)} %cotangent.3, f32[8,4096]{1,0:T(8,128)} %decay.11), custom_call_target="tpu_custom_call" | custom-call | tf_op jit(solution)/shard_map/local/pallas_call | solution.py:240
  9.7 18.5 %all_to_all.25.data = f32[4,384,128]{2,1,0:T(8,128)S(1)} all-to-all(f32[4,384,128]{2,1,0:T(8,128)S(1)} %bitcast.4), channel_id=1, replica_groups={{0,1,2,3},{4,5,6,7},{8,9,10,11},{12,13,14,15},{16,17,18,19},{20,21,22,2..., dimensions={0} | all-to-all | bytes 1572864 | tf_op jit(solution)/shard_map/all_to_all | solution.py:251
  28.2 0.0 copy-done
  28.2 0.8 near.1
  28.9 31.0 %all_to_all.26.data = f32[8,48,128]{2,1,0:T(8,128)S(1)} all-to-all(f32[8,48,128]{2,1,0:T(8,128)S(1)} %get-tuple-element.13), channel_id=1, replica_groups={{0,4,8,12,16,20,24,28},{1,5,9,13,17,21,25,29},{2,6,10,14,18,22,26,30},{..., dimensions={0} | all-to-all | bytes 393216 | tf_op jit(solution)/shard_map/all_to_all | solution.py:251
  60.0 0.7 far.1
  60.7 9.1 %all_to_all.27.sums = f32[16,16,128]{2,1,0:T(8,128)S(1)} all-to-all(f32[16,16,128]{2,1,0:T(8,128)S(1)} %get-tuple-element.15), channel_id=1, replica_groups=mesh['dp'=16,'ctx'=32] {'dp'}, dimensions={0} | all-to-all | bytes 262144 | tf_op jit(solution)/shard_map/all_to_all | solution.py:251
  69.7 0.7 sum.1
  70.4 3.4 %all-to-all-start.3 = ((f32[8,24,128]{2,1,0:T(8,128)}), f32[8,24,128]{2,1,0:T(8,128)S(1)}, u32[]{:S(2)}, u32[]{:S(2)}) async-start(f32[8,24,128]{2,1,0:T(8,128)} %sum.1), calls=%async_computation.3 | async-start | bytes 196608 | tf_op jit(solution)/shard_map/all_to_all | solution.py:251
  73.8 0.0 copy-start.1
  73.8 0.0 copy-start.2
  73.8 5.3 %inner.1 = f32[128,4096]{1,0:T(8,128)S(1)} custom-call(bf16[1,128,4096]{2,1,0:T(8,128)(2,1)} %gate.3, bf16[1,128,4096]{2,1,0:T(8,128)(2,1)} %cotangent.3, f32[8,4096]{1,0:T(8,128)} %decay.11, f32[8,4096]{1,0:T(8,128)} %residues.3), custom_call_target="tpu_custom_call" | custom-call | flops 16777216 | bytes 4194304 | tf_op jit(solution)/shard_map/inner/pallas_call | solution.py:254
  79.1 9.4 %all-to-all-done.3.far = f32[8,24,128]{2,1,0:T(8,128)S(1)} async-done(((f32[8,24,128]{2,1,0:T(8,128)}), f32[8,24,128]{2,1,0:T(8,128)S(1)}, u32[]{:S(2)}, u32[]{:S(2)}) %all-to-all-start.3) | async-done | bytes 98336 | tf_op jit(solution)/shard_map/all_to_all | solution.py:251
  88.5 0.0 copy-done.1
  88.5 0.7 spread.1
  89.2 11.1 %all_to_all.28 = f32[4,192,128]{2,1,0:T(8,128)S(1)} all-to-all(f32[4,192,128]{2,1,0:T(8,128)S(1)} %spread.1), channel_id=1, replica_groups={{0,1,2,3},{4,5,6,7},{8,9,10,11},{12,13,14,15},{16,17,18,19},{20,21,22,2..., dimensions={0} | all-to-all | bytes 786432 | tf_op jit(solution)/shard_map/all_to_all | solution.py:251
  100.4 0.0 copy-done.2
  100.4 2.3 %final.1 = (bf16[1,128,4096]{2,1,0:T(8,128)(2,1)}, f32[8,4096]{1,0:T(8,128)}, f32[8,4096]{1,0:T(8,128)}) custom-call(f32[128,4096]{1,0:T(8,128)S(1)} %inner.1, f32[768,128]{1,0:T(8,128)S(1)} %bitcast.5, f32[8,4096]{1,0:T(8,128)S(1)} %copy-done.1, f32[8,4096]{1,0:T(8,128)S(1)} %copy-done.2), custom_call_target="tpu_custom_call" | custom-call | tf_op jit(solution)/shard_map/final/pallas_call | solution.py:308
Async XLA Ops:
  1.2 26.9 %copy-start = (f32[8,4096]{1,0:T(8,128)S(1)}, f32[8,4096]{1,0:T(8,128)}, u32[]{:S(2)}) copy-start(f32[8,4096]{1,0:T(8,128)} %decay.11) | copy-start | bytes 393220
  70.4 18.1 %all-to-all-start.3 = ((f32[8,24,128]{2,1,0:T(8,128)}), f32[8,24,128]{2,1,0:T(8,128)S(1)}, u32[]{:S(2)}, u32[]{:S(2)}) async-start(f32[8,24,128]{2,1,0:T(8,128)} %sum.1), calls=%async_computation.3 | async-start | bytes 196608 | tf_op jit(solution)/shard_map/all_to_all | solution.py:251
  73.8 14.7 %copy-start.1 = (f32[8,4096]{1,0:T(8,128)S(1)}, f32[8,4096]{1,0:T(8,128)}, u32[]{:S(2)}) copy-start(f32[8,4096]{1,0:T(8,128)} %decay.11) | copy-start | bytes 393220
  73.8 26.6 %copy-start.2 = (f32[8,4096]{1,0:T(8,128)S(1)}, f32[8,4096]{1,0:T(8,128)}, u32[]{:S(2)}) copy-start(f32[8,4096]{1,0:T(8,128)} %residues.3) | copy-start | bytes 393220

commit v7 on v6

--- a/solution.py
+++ b/solution.py
@@ -97,9 +97,9 @@
     return carries[::-1], (all_state, all_moment, carry, ramp, total0, total1)
 
 
-def near_kernel(span, modes, place, decay, data, totals, carries):
+def near_kernel(span, modes, decay, data, totals, carries):
     height = SENT * modes
-    first = place[0] * WIDE
+    first = lax.rem(lax.axis_index("ctx"), NEAR) * WIDE
     for tile in range(SUBS):
         part = lambda b, k: data[b, tile * height + k * modes : tile * height + (k + 1) * modes, :]
         here = decay[:, pl.ds(pl.multiple_of(first + tile * LANES, LANES), LANES)]
@@ -111,8 +111,10 @@
             totals[tile, k * modes : (k + 1) * modes, :] = total[k]
 
 
-def far_kernel(span, modes, place, decay, data, carries, sums):
-    here = decay[:, pl.ds(pl.multiple_of(place[1] * LANES, LANES), LANES)]
+def far_kernel(span, modes, decay, data, carries, sums):
+    me = lax.axis_index("ctx")
+    tile = lax.rem(me, NEAR) * SUBS + lax.div(me, NEAR)
+    here = decay[:, pl.ds(pl.multiple_of(tile * LANES, LANES), LANES)]
     blocks = [
         [data[b, k * modes : (k + 1) * modes, :] for k in range(SENT)] for b in range(data.shape[0])
     ]
@@ -133,9 +135,9 @@
         out[b, modes:, :] = total
 
 
-def spread_kernel(span, modes, place, decay, carries, far, out):
+def spread_kernel(span, modes, decay, carries, far, out):
     height = BACK * modes
-    first = place[0] * WIDE
+    first = lax.rem(lax.axis_index("ctx"), NEAR) * WIDE
     blocks = carries.shape[0]
     for tile in range(SUBS):
         here = decay[:, pl.ds(pl.multiple_of(first + tile * LANES, LANES), LANES)]
@@ -221,14 +223,10 @@
     far = peers // NEAR
     wide = channels // WIDE
     assert modes == SUBS and wide == NEAR and far == SUBS and values.shape[0] == 1
-    me = lax.axis_index("ctx")
-    place = jnp.stack([me % NEAR, (me % NEAR) * SUBS + me // NEAR]).astype(jnp.int32)
-    place, values = lax.optimization_barrier((place, values))
     near_groups = [[g * NEAR + k for k in range(NEAR)] for g in range(far)]
     far_groups = [[k * NEAR + g for k in range(far)] for g in range(NEAR)]
     shape = lambda *dims: jax.ShapeDtypeStruct(dims, F32)
     vmem = pl.BlockSpec(memory_space=pltpu.VMEM)
-    smem = pl.BlockSpec(memory_space=pltpu.SMEM)
     on_chip = lambda x: pltpu.with_memory_space_constraint(x, pltpu.VMEM)
     held = lambda *dims: pltpu.VMEM(dims, F32)
 
@@ -269,20 +267,20 @@
     )(gate_values, cotangent, decay_rates, residues)
     totals, near_carries = pl.pallas_call(
         functools.partial(near_kernel, float(length), modes),
-        in_specs=[smem, vmem, vmem],
+        in_specs=[vmem, vmem],
         out_specs=[vmem, vmem],
         out_shape=[held(far, SENT * modes, LANES), held(NEAR, SUBS * modes, LANES)],
         name="near",
-    )(place, near_decay, on_chip(near_data))
+    )(near_decay, on_chip(near_data))
 
     far_data = exchange(totals, "ctx", far_groups)
     far_carries, sums = pl.pallas_call(
         functools.partial(far_kernel, float(length * NEAR), modes),
-        in_specs=[smem, vmem, vmem],
+        in_specs=[vmem, vmem],
         out_specs=[vmem, vmem],
         out_shape=[held(far, modes, LANES), held(rows_of, 2 * modes, LANES)],
         name="far",
-    )(place, near_decay, on_chip(far_data))
+    )(near_decay, on_chip(far_data))
 
     all_sums = exchange(sums, "dp", None)
     far_out = pl.pallas_call(
@@ -297,11 +295,11 @@
     far_back, inner = lax.optimization_barrier((far_back, inner))
     near_out = pl.pallas_call(
         functools.partial(spread_kernel, float(length), modes),
-        in_specs=[smem, vmem, vmem, vmem],
+        in_specs=[vmem, vmem, vmem],
         out_specs=vmem,
         out_shape=held(NEAR, SUBS * BACK * modes, LANES),
         name="spread",
-    )(place, near_decay, on_chip(near_carries), on_chip(far_back))
+    )(near_decay, on_chip(near_carries), on_chip(far_back))
 
     arrived = exchange(near_out, "ctx", near_groups)
     scale = 1.0 / math.sqrt(rows_of * length * peers)

time: 104 us -> 101 us (0.971)
  Pallas kernels: 18.8 us -> 16.9 us
where the time goes in v7:
time: 101 us; the launch traced here: 100 us
  blocking collectives  69.7 us (69%)
  Pallas kernels  16.9 us (17%)
  waiting for transfers between devices  9.45 us (9%)
  starting transfers between devices  3.36 us (3%)
    all_to_all x4, blocking collectives, exchange(): return lax.all_to_all(x, axis, 0, 0, tiled=True, axis_index_groups=groups)  69.7 us
    all_to_all x1, waiting for transfers between devices, exchange(): return lax.all_to_all(x, axis, 0, 0, tiled=True, axis_index_groups=groups)  9.45 us
    pallas_call x1, Pallas kernels, on_device(): pl.pallas_call(functools.partial(local_kernel, length, modes), grid=(wide...  8.48 us
    pallas_call x1, Pallas kernels, on_device(): pl.pallas_call(functools.partial(inner_kernel, length, modes), grid=(wide...  5.26 us
    all_to_all x1, starting transfers between devices, exchange(): return lax.all_to_all(x, axis, 0, 0, tiled=True, axis_index_groups=groups)  3.36 us
    pallas_call x1, Pallas kernels, on_device(): pl.pallas_call(functools.partial(final_kernel, length, modes, scale), gri...  2.28 us
  transfers between devices with their start and end apart: 1, of which 1 were waited for; matrix products, arithmetic and copies ran while one was open for 0% of the time, Pallas kernels for 5%

profile of v7, /device:TPU:6, one launch (start us, length us, event | category | flops | bytes accessed | tf_op | source)
XLA Modules:
  0.0 100.1 jit_solution(13918369628078503556)
XLA Ops:
  0.6 0.0 copy-start
  0.6 8.5 %local.1 = f32[1536,128]{1,0:T(8,128)S(1)} custom-call(bf16[1,128,4096]{2,1,0:T(8,128)(2,1)} %values.1, bf16[1,128,4096]{2,1,0:T(8,128)(2,1)} %gate.3, bf16[1,128,4096]{2,1,0:T(8,128)(2,1)} %cotangent.3, f32[8,4096]{1,0:T(8,128)} %decay.11), custom_call_target="tpu_custom_call" | custom-call | tf_op jit(solution)/shard_map/local/pallas_call | solution.py:238
  9.1 18.5 %all_to_all.25.data = f32[4,384,128]{2,1,0:T(8,128)S(1)} all-to-all(f32[4,384,128]{2,1,0:T(8,128)S(1)} %bitcast.2), channel_id=1, replica_groups={{0,1,2,3},{4,5,6,7},{8,9,10,11},{12,13,14,15},{16,17,18,19},{20,21,22,2..., dimensions={0} | all-to-all | bytes 1572864 | tf_op jit(solution)/shard_map/all_to_all | solution.py:249
  27.6 0.0 copy-done
  27.6 0.1 near.1
  27.7 31.0 %all_to_all.26.data = f32[8,48,128]{2,1,0:T(8,128)S(1)} all-to-all(f32[8,48,128]{2,1,0:T(8,128)S(1)} %get-tuple-element.9), channel_id=1, replica_groups={{0,4,8,12,16,20,24,28},{1,5,9,13,17,21,25,29},{2,6,10,14,18,22,26,30},{..., dimensions={0} | all-to-all | bytes 393216 | tf_op jit(solution)/shard_map/all_to_all | solution.py:249
  58.8 9.1 %all_to_all.27.sums = f32[16,16,128]{2,1,0:T(8,128)S(1)} all-to-all(f32[16,16,128]{2,1,0:T(8,128)S(1)} %get-tuple-element.11), channel_id=1, replica_groups=mesh['dp'=16,'ctx'=32] {'dp'}, dimensions={0} | all-to-all | bytes 262144 | tf_op jit(solution)/shard_map/all_to_all | solution.py:249
  67.8 0.7 sum.1
  68.5 3.4 %all-to-all-start.3 = ((f32[8,24,128]{2,1,0:T(8,128)}), f32[8,24,128]{2,1,0:T(8,128)S(1)}, u32[]{:S(2)}, u32[]{:S(2)}) async-start(f32[8,24,128]{2,1,0:T(8,128)} %sum.1), calls=%async_computation.3 | async-start | bytes 196608 | tf_op jit(solution)/shard_map/all_to_all | solution.py:249
  71.9 0.0 copy-start.1
  71.9 0.0 copy-start.2
  71.9 5.3 %inner.1 = f32[128,4096]{1,0:T(8,128)S(1)} custom-call(bf16[1,128,4096]{2,1,0:T(8,128)(2,1)} %gate.3, bf16[1,128,4096]{2,1,0:T(8,128)(2,1)} %cotangent.3, f32[8,4096]{1,0:T(8,128)} %decay.11, f32[8,4096]{1,0:T(8,128)} %residues.3), custom_call_target="tpu_custom_call" | custom-call | flops 16777216 | bytes 4194304 | tf_op jit(solution)/shard_map/inner/pallas_call | solution.py:252
  77.2 9.4 %all-to-all-done.3.far = f32[8,24,128]{2,1,0:T(8,128)S(1)} async-done(((f32[8,24,128]{2,1,0:T(8,128)}), f32[8,24,128]{2,1,0:T(8,128)S(1)}, u32[]{:S(2)}, u32[]{:S(2)}) %all-to-all-start.3) | async-done | bytes 98336 | tf_op jit(solution)/shard_map/all_to_all | solution.py:249
  86.6 0.0 copy-done.1
  86.7 11.1 %all_to_all.28 = f32[4,192,128]{2,1,0:T(8,128)S(1)} all-to-all(f32[4,192,128]{2,1,0:T(8,128)S(1)} %spread.1), channel_id=1, replica_groups={{0,1,2,3},{4,5,6,7},{8,9,10,11},{12,13,14,15},{16,17,18,19},{20,21,22,2..., dimensions={0} | all-to-all | bytes 786432 | tf_op jit(solution)/shard_map/all_to_all | solution.py:249
  97.8 0.0 copy-done.2
  97.8 2.3 %final.1 = (bf16[1,128,4096]{2,1,0:T(8,128)(2,1)}, f32[8,4096]{1,0:T(8,128)}, f32[8,4096]{1,0:T(8,128)}) custom-call(f32[128,4096]{1,0:T(8,128)S(1)} %inner.1, f32[768,128]{1,0:T(8,128)S(1)} %bitcast.3, f32[8,4096]{1,0:T(8,128)S(1)} %copy-done.1, f32[8,4096]{1,0:T(8,128)S(1)} %copy-done.2), custom_call_target="tpu_custom_call" | custom-call | tf_op jit(solution)/shard_map/final/pallas_call | solution.py:306
  (2 shorter events, 0.1 us)
Async XLA Ops:
  0.6 27.0 %copy-start = (f32[8,4096]{1,0:T(8,128)S(1)}, f32[8,4096]{1,0:T(8,128)}, u32[]{:S(2)}) copy-start(f32[8,4096]{1,0:T(8,128)} %decay.11) | copy-start | bytes 393220
  68.5 18.1 %all-to-all-start.3 = ((f32[8,24,128]{2,1,0:T(8,128)}), f32[8,24,128]{2,1,0:T(8,128)S(1)}, u32[]{:S(2)}, u32[]{:S(2)}) async-start(f32[8,24,128]{2,1,0:T(8,128)} %sum.1), calls=%async_computation.3 | async-start | bytes 196608 | tf_op jit(solution)/shard_map/all_to_all | solution.py:249
  71.9 14.7 %copy-start.1 = (f32[8,4096]{1,0:T(8,128)S(1)}, f32[8,4096]{1,0:T(8,128)}, u32[]{:S(2)}) copy-start(f32[8,4096]{1,0:T(8,128)} %decay.11) | copy-start | bytes 393220
  71.9 25.9 %copy-start.2 = (f32[8,4096]{1,0:T(8,128)S(1)}, f32[8,4096]{1,0:T(8,128)}, u32[]{:S(2)}) copy-start(f32[8,4096]{1,0:T(8,128)} %residues.3) | copy-start | bytes 393220

commit v8 on v7

--- a/solution.py
+++ b/solution.py
@@ -283,6 +283,7 @@
     )(near_decay, on_chip(far_data))
 
     all_sums = exchange(sums, "dp", None)
+    all_sums, inner = lax.optimization_barrier((all_sums, inner))
     far_out = pl.pallas_call(
         functools.partial(sum_kernel, modes),
         in_specs=[vmem, vmem],
@@ -292,7 +293,6 @@
     )(on_chip(far_carries), on_chip(all_sums))
 
     far_back = exchange(far_out, "ctx", far_groups)
-    far_back, inner = lax.optimization_barrier((far_back, inner))
     near_out = pl.pallas_call(
         functools.partial(spread_kernel, float(length), modes),
         in_specs=[vmem, vmem, vmem],

time: 101 us -> 101 us (level)
  waiting for transfers between devices: 9.45 us -> 0.01 us
  blocking collectives: 69.7 us -> 77.9 us
  starting transfers between devices: 3.36 us -> 4.91 us
    all_to_all x1, waiting for transfers between devices: 9.45 us -> 0.01 us  [exchange(): return lax.all_to_all(x, axis, 0, 0, tiled=True, axis_index_groups=groups)]
    all_to_all x4, blocking collectives: 69.7 us -> 77.9 us  [exchange(): return lax.all_to_all(x, axis, 0, 0, tiled=True, axis_index_groups=groups)]
    all_to_all x1, starting transfers between devices: 3.36 us -> 4.91 us  [exchange(): return lax.all_to_all(x, axis, 0, 0, tiled=True, axis_index_groups=groups)]
  transfers between devices with their start and end apart: 1 -> 1, of which waited for: 1 -> 0; matrix products, arithmetic and copies ran while one was open for 0% -> 0% of each run, Pallas kernels for 5% -> 5%
where the time goes in v8:
time: 101 us; the launch traced here: 100 us
  blocking collectives  77.9 us (77%)
  Pallas kernels  16.9 us (17%)
  starting transfers between devices  4.91 us (5%)
    all_to_all x4, blocking collectives, exchange(): return lax.all_to_all(x, axis, 0, 0, tiled=True, axis_index_groups=groups)  77.9 us
    pallas_call x1, Pallas kernels, on_device(): pl.pallas_call(functools.partial(local_kernel, length, modes), grid=(wide...  8.48 us
    pallas_call x1, Pallas kernels, on_device(): pl.pallas_call(functools.partial(inner_kernel, length, modes), grid=(wide...  5.26 us
    all_to_all x1, starting transfers between devices, exchange(): return lax.all_to_all(x, axis, 0, 0, tiled=True, axis_index_groups=groups)  4.91 us
    pallas_call x1, Pallas kernels, on_device(): pl.pallas_call(functools.partial(final_kernel, length, modes, scale), gri...  2.28 us
  transfers between devices with their start and end apart: 1, of which 0 were waited for; matrix products, arithmetic and copies ran while one was open for 0% of the time, Pallas kernels for 5%

profile of v8, /device:TPU:6, one launch (start us, length us, event | category | flops | bytes accessed | tf_op | source)
XLA Modules:
  0.0 100.4 jit_solution(111604112121244084)
XLA Ops:
  0.6 0.0 copy-start
  0.6 8.5 %local.1 = f32[1536,128]{1,0:T(8,128)S(1)} custom-call(bf16[1,128,4096]{2,1,0:T(8,128)(2,1)} %values.1, bf16[1,128,4096]{2,1,0:T(8,128)(2,1)} %gate.3, bf16[1,128,4096]{2,1,0:T(8,128)(2,1)} %cotangent.3, f32[8,4096]{1,0:T(8,128)} %decay.11), custom_call_target="tpu_custom_call" | custom-call | tf_op jit(solution)/shard_map/local/pallas_call | solution.py:238
  9.1 18.5 %all_to_all.25.data = f32[4,384,128]{2,1,0:T(8,128)S(1)} all-to-all(f32[4,384,128]{2,1,0:T(8,128)S(1)} %bitcast.2), channel_id=1, replica_groups={{0,1,2,3},{4,5,6,7},{8,9,10,11},{12,13,14,15},{16,17,18,19},{20,21,22,2..., dimensions={0} | all-to-all | bytes 1572864 | tf_op jit(solution)/shard_map/all_to_all | solution.py:249
  27.6 0.0 copy-done
  27.6 0.1 near.1
  27.7 31.0 %all_to_all.26.data = f32[8,48,128]{2,1,0:T(8,128)S(1)} all-to-all(f32[8,48,128]{2,1,0:T(8,128)S(1)} %get-tuple-element.9), channel_id=1, replica_groups={{0,4,8,12,16,20,24,28},{1,5,9,13,17,21,25,29},{2,6,10,14,18,22,26,30},{..., dimensions={0} | all-to-all | bytes 393216 | tf_op jit(solution)/shard_map/all_to_all | solution.py:249
  58.7 0.7 far.1
  59.4 4.9 %all-to-all-start.2 = ((f32[16,16,128]{2,1,0:T(8,128)}), f32[16,16,128]{2,1,0:T(8,128)S(1)}, u32[]{:S(2)}, u32[]{:S(2)}) async-start(f32[16,16,128]{2,1,0:T(8,128)} %get-tuple-element.10), calls=%async_computation.2 | async-start | bytes 262144 | tf_op jit(solution)/shard_map/all_to_all | solution.py:249
  64.3 0.0 copy-start.1
  64.3 0.0 copy-start.2
  64.4 5.3 %inner.1 = f32[128,4096]{1,0:T(8,128)S(1)} custom-call(bf16[1,128,4096]{2,1,0:T(8,128)(2,1)} %gate.3, bf16[1,128,4096]{2,1,0:T(8,128)(2,1)} %cotangent.3, f32[8,4096]{1,0:T(8,128)} %decay.11, f32[8,4096]{1,0:T(8,128)} %residues.3), custom_call_target="tpu_custom_call" | custom-call | flops 16777216 | bytes 4194304 | tf_op jit(solution)/shard_map/inner/pallas_call | solution.py:252
  69.6 0.0 all-to-all-done.2.sums
  69.7 17.8 %all_to_all.27.far = f32[8,24,128]{2,1,0:T(8,128)S(1)} all-to-all(f32[8,24,128]{2,1,0:T(8,128)S(1)} %sum.1), channel_id=1, replica_groups={{0,4,8,12,16,20,24,28},{1,5,9,13,17,21,25,29},{2,6,10,14,18,22,26,30},{..., dimensions={0} | all-to-all | bytes 196608 | tf_op jit(solution)/shard_map/all_to_all | solution.py:249
  87.5 0.0 copy-done.1
  87.5 10.6 %all_to_all.28 = f32[4,192,128]{2,1,0:T(8,128)S(1)} all-to-all(f32[4,192,128]{2,1,0:T(8,128)S(1)} %spread.1), channel_id=1, replica_groups={{0,1,2,3},{4,5,6,7},{8,9,10,11},{12,13,14,15},{16,17,18,19},{20,21,22,2..., dimensions={0} | all-to-all | bytes 786432 | tf_op jit(solution)/shard_map/all_to_all | solution.py:249
  98.2 0.0 copy-done.2
  98.2 2.3 %final.1 = (bf16[1,128,4096]{2,1,0:T(8,128)(2,1)}, f32[8,4096]{1,0:T(8,128)}, f32[8,4096]{1,0:T(8,128)}) custom-call(f32[128,4096]{1,0:T(8,128)S(1)} %inner.1, f32[768,128]{1,0:T(8,128)S(1)} %bitcast.3, f32[8,4096]{1,0:T(8,128)S(1)} %copy-done.1, f32[8,4096]{1,0:T(8,128)S(1)} %copy-done.2), custom_call_target="tpu_custom_call" | custom-call | tf_op jit(solution)/shard_map/final/pallas_call | solution.py:306
  (2 shorter events, 0.1 us)
Async XLA Ops:
  0.6 27.0 %copy-start = (f32[8,4096]{1,0:T(8,128)S(1)}, f32[8,4096]{1,0:T(8,128)}, u32[]{:S(2)}) copy-start(f32[8,4096]{1,0:T(8,128)} %decay.11) | copy-start | bytes 393220
  59.4 10.2 %all-to-all-start.2 = ((f32[16,16,128]{2,1,0:T(8,128)}), f32[16,16,128]{2,1,0:T(8,128)S(1)}, u32[]{:S(2)}, u32[]{:S(2)}) async-start(f32[16,16,128]{2,1,0:T(8,128)} %get-tuple-element.10), calls=%async_computation.2 | async-start | bytes 262144 | tf_op jit(solution)/shard_map/all_to_all | solution.py:249
  64.3 23.1 %copy-start.1 = (f32[8,4096]{1,0:T(8,128)S(1)}, f32[8,4096]{1,0:T(8,128)}, u32[]{:S(2)}) copy-start(f32[8,4096]{1,0:T(8,128)} %decay.11) | copy-start | bytes 393220
  64.3 33.8 %copy-start.2 = (f32[8,4096]{1,0:T(8,128)S(1)}, f32[8,4096]{1,0:T(8,128)}, u32[]{:S(2)}) copy-start(f32[8,4096]{1,0:T(8,128)} %residues.3) | copy-start | bytes 393220

commit v9 on v8

--- a/solution.py
+++ b/solution.py
@@ -274,6 +274,7 @@
     )(near_decay, on_chip(near_data))
 
     far_data = exchange(totals, "ctx", far_groups)
+    far_data, inner = lax.optimization_barrier((far_data, inner))
     far_carries, sums = pl.pallas_call(
         functools.partial(far_kernel, float(length * NEAR), modes),
         in_specs=[vmem, vmem],
@@ -283,7 +284,6 @@
     )(near_decay, on_chip(far_data))
 
     all_sums = exchange(sums, "dp", None)
-    all_sums, inner = lax.optimization_barrier((all_sums, inner))
     far_out = pl.pallas_call(
         functools.partial(sum_kernel, modes),
         in_specs=[vmem, vmem],

time: 101 us -> 101 us (level)
  blocking collectives: 77.9 us -> 56 us
  waiting for transfers between devices: 0.01 us -> 11.8 us
  starting transfers between devices: 4.91 us -> 14.2 us
    all_to_all x4, blocking collectives: 77.9 us -> 56 us  [exchange(): return lax.all_to_all(x, axis, 0, 0, tiled=True, axis_index_groups=groups)]
    all_to_all x1, waiting for transfers between devices: 0.01 us -> 11.8 us  [exchange(): return lax.all_to_all(x, axis, 0, 0, tiled=True, axis_index_groups=groups)]
    all_to_all x1, starting transfers between devices: 4.91 us -> 14.2 us  [exchange(): return lax.all_to_all(x, axis, 0, 0, tiled=True, axis_index_groups=groups)]
  transfers between devices with their start and end apart: 1 -> 1, of which waited for: 0 -> 1; matrix products, arithmetic and copies ran while one was open for 0% -> 0% of each run, Pallas kernels for 5% -> 5%
where the time goes in v9:
time: 101 us; the launch traced here: 99.5 us
  blocking collectives  56 us (55%)
  Pallas kernels  16.9 us (17%)
  starting transfers between devices  14.2 us (14%)
  waiting for transfers between devices  11.8 us (12%)
    all_to_all x4, blocking collectives, exchange(): return lax.all_to_all(x, axis, 0, 0, tiled=True, axis_index_groups=groups)  56 us
    all_to_all x1, starting transfers between devices, exchange(): return lax.all_to_all(x, axis, 0, 0, tiled=True, axis_index_groups=groups)  14.2 us
    all_to_all x1, waiting for transfers between devices, exchange(): return lax.all_to_all(x, axis, 0, 0, tiled=True, axis_index_groups=groups)  11.8 us
    pallas_call x1, Pallas kernels, on_device(): pl.pallas_call(functools.partial(local_kernel, length, modes), grid=(wide...  8.48 us
    pallas_call x1, Pallas kernels, on_device(): pl.pallas_call(functools.partial(inner_kernel, length, modes), grid=(wide...  5.22 us
    pallas_call x1, Pallas kernels, on_device(): pl.pallas_call(functools.partial(final_kernel, length, modes, scale), gri...  2.28 us
  transfers between devices with their start and end apart: 1, of which 1 were waited for; matrix products, arithmetic and copies ran while one was open for 0% of the time, Pallas kernels for 5%

profile of v9, /device:TPU:6, one launch (start us, length us, event | category | flops | bytes accessed | tf_op | source)
XLA Modules:
  0.0 99.5 jit_solution(7036143557832303621)
XLA Ops:
  0.6 0.0 copy-start
  0.6 8.5 %local.1 = f32[1536,128]{1,0:T(8,128)S(1)} custom-call(bf16[1,128,4096]{2,1,0:T(8,128)(2,1)} %values.1, bf16[1,128,4096]{2,1,0:T(8,128)(2,1)} %gate.3, bf16[1,128,4096]{2,1,0:T(8,128)(2,1)} %cotangent.3, f32[8,4096]{1,0:T(8,128)} %decay.11), custom_call_target="tpu_custom_call" | custom-call | tf_op jit(solution)/shard_map/local/pallas_call | solution.py:238
  9.1 18.5 %all_to_all.25.data = f32[4,384,128]{2,1,0:T(8,128)S(1)} all-to-all(f32[4,384,128]{2,1,0:T(8,128)S(1)} %bitcast.2), channel_id=1, replica_groups={{0,1,2,3},{4,5,6,7},{8,9,10,11},{12,13,14,15},{16,17,18,19},{20,21,22,2..., dimensions={0} | all-to-all | bytes 1572864 | tf_op jit(solution)/shard_map/all_to_all | solution.py:249
  27.6 0.0 copy-done
  27.6 0.8 near.1
  28.4 14.2 %all-to-all-start.1 = ((f32[8,48,128]{2,1,0:T(8,128)}), f32[8,48,128]{2,1,0:T(8,128)S(1)}, u32[]{:S(2)}, u32[]{:S(2)}) async-start(f32[8,48,128]{2,1,0:T(8,128)} %get-tuple-element.9), calls=%async_computation.1 | async-start | bytes 393216 | tf_op jit(solution)/shard_map/all_to_all | solution.py:249
  42.6 0.0 copy-start.1
  42.6 5.2 %inner.1 = f32[128,4096]{1,0:T(8,128)S(1)} custom-call(bf16[1,128,4096]{2,1,0:T(8,128)(2,1)} %gate.3, bf16[1,128,4096]{2,1,0:T(8,128)(2,1)} %cotangent.3, f32[8,4096]{1,0:T(8,128)} %decay.11, f32[8,4096]{1,0:T(8,128)} %residues.3), custom_call_target="tpu_custom_call" | custom-call | flops 16777216 | bytes 4194304 | tf_op jit(solution)/shard_map/inner/pallas_call | solution.py:252
  47.8 0.0 copy-start.2
  47.8 11.8 %all-to-all-done.1.data = f32[8,48,128]{2,1,0:T(8,128)S(1)} async-done(((f32[8,48,128]{2,1,0:T(8,128)}), f32[8,48,128]{2,1,0:T(8,128)S(1)}, u32[]{:S(2)}, u32[]{:S(2)}) %all-to-all-start.1) | async-done | bytes 196640 | tf_op jit(solution)/shard_map/all_to_all | solution.py:249
  59.6 0.0 copy-done.1
  59.6 9.1 %all_to_all.26.sums = f32[16,16,128]{2,1,0:T(8,128)S(1)} all-to-all(f32[16,16,128]{2,1,0:T(8,128)S(1)} %get-tuple-element.14), channel_id=1, replica_groups=mesh['dp'=16,'ctx'=32] {'dp'}, dimensions={0} | all-to-all | bytes 262144 | tf_op jit(solution)/shard_map/all_to_all | solution.py:249
  68.7 17.8 %all_to_all.27.far = f32[8,24,128]{2,1,0:T(8,128)S(1)} all-to-all(f32[8,24,128]{2,1,0:T(8,128)S(1)} %sum.1), channel_id=1, replica_groups={{0,4,8,12,16,20,24,28},{1,5,9,13,17,21,25,29},{2,6,10,14,18,22,26,30},{..., dimensions={0} | all-to-all | bytes 196608 | tf_op jit(solution)/shard_map/all_to_all | solution.py:249
  86.6 10.6 %all_to_all.28 = f32[4,192,128]{2,1,0:T(8,128)S(1)} all-to-all(f32[4,192,128]{2,1,0:T(8,128)S(1)} %spread.1), channel_id=1, replica_groups={{0,1,2,3},{4,5,6,7},{8,9,10,11},{12,13,14,15},{16,17,18,19},{20,21,22,2..., dimensions={0} | all-to-all | bytes 786432 | tf_op jit(solution)/shard_map/all_to_all | solution.py:249
  97.2 0.0 copy-done.2
  97.2 2.3 %final.1 = (bf16[1,128,4096]{2,1,0:T(8,128)(2,1)}, f32[8,4096]{1,0:T(8,128)}, f32[8,4096]{1,0:T(8,128)}) custom-call(f32[128,4096]{1,0:T(8,128)S(1)} %inner.1, f32[768,128]{1,0:T(8,128)S(1)} %bitcast.3, f32[8,4096]{1,0:T(8,128)S(1)} %copy-done.1, f32[8,4096]{1,0:T(8,128)S(1)} %copy-done.2), custom_call_target="tpu_custom_call" | custom-call | tf_op jit(solution)/shard_map/final/pallas_call | solution.py:306
  (3 shorter events, 0.1 us)
Async XLA Ops:
  0.6 27.0 %copy-start = (f32[8,4096]{1,0:T(8,128)S(1)}, f32[8,4096]{1,0:T(8,128)}, u32[]{:S(2)}) copy-start(f32[8,4096]{1,0:T(8,128)} %decay.11) | copy-start | bytes 393220
  28.4 31.2 %all-to-all-start.1 = ((f32[8,48,128]{2,1,0:T(8,128)}), f32[8,48,128]{2,1,0:T(8,128)S(1)}, u32[]{:S(2)}, u32[]{:S(2)}) async-start(f32[8,48,128]{2,1,0:T(8,128)} %get-tuple-element.9), calls=%async_computation.1 | async-start | bytes 393216 | tf_op jit(solution)/shard_map/all_to_all | solution.py:249
  42.6 17.0 %copy-start.1 = (f32[8,4096]{1,0:T(8,128)S(1)}, f32[8,4096]{1,0:T(8,128)}, u32[]{:S(2)}) copy-start(f32[8,4096]{1,0:T(8,128)} %decay.11) | copy-start | bytes 393220
  47.8 49.4 %copy-start.2 = (f32[8,4096]{1,0:T(8,128)S(1)}, f32[8,4096]{1,0:T(8,128)}, u32[]{:S(2)}) copy-start(f32[8,4096]{1,0:T(8,128)} %residues.3) | copy-start | bytes 393220
